TPU v7x, 32 devices: a whole 2x2x4 slice. The times are simulated.
32 devices in a mesh: vocab: 8 (over y, x, core), dp: 4 (over z).
Axes of the slice: x: 2, y: 2, z: 4, core: 2. Of those that a mesh axis runs over, the one named last changes fastest.
Arguments:
- token_ids: int32 [32768], P(('vocab', 'dp')), may hold values from 0 to 262143, as said below
- counts: int32 [32], P(('vocab', 'dp')), may hold values from 256 to 1024, as said below
- table: bfloat16 [262144, 128], P(('vocab', 'dp')), may hold values from -6 to 6
- projection: bfloat16 [128, 4096], replicated, may hold values from -0.5 to 0.5
- cotangent: bfloat16 [32768, 4096], P(('vocab', 'dp')), may hold values from -4 to 4
Outputs:
- hidden: bfloat16 [32768, 4096], P(('vocab', 'dp'))
- grad_projection: float32 [128, 4096], replicated
- grad_table: float32 [262144, 128], P(('vocab', 'dp'))
Inputs may be any that keep to these rules, and one draw needn't show every extreme that they name: `token_ids`: on each device at most 64 tokens have ids in the rows of any one device, and in every draw one device's rows receive exactly 64 tokens from every device; which rows are frequent is drawn from the seed. `counts`: in every draw some device has all 1024 tokens live.
All inputs are finite; a program needn't handle non-finite values.
Results may differ from a plain program's by a relative error of at most 0.0029.
Values may be sent and summed in bfloat16 or wider, within the bound.
A program may use at most 128 MiB of HBM per device.

v0:
```python
import math

import jax
import jax.numpy as jnp
from jax import lax
from jax.sharding import PartitionSpec as P


def move_ids(requests):
    return lax.all_to_all(requests, ("vocab", "dp"), split_axis=0, concat_axis=0, tiled=True)


def move_rows(blocks):
    return lax.all_to_all(blocks, ("vocab", "dp"), split_axis=0, concat_axis=0, tiled=True)


def sum_projection(terms, scaling):
    return lax.psum(terms, ("vocab", "dp")) * scaling


def body(token_ids, counts, table, projection, cotangent):
    tokens_here = token_ids.shape[0]
    held_rows = table.shape[0]
    width = table.shape[1]
    n_vocab = lax.axis_size("vocab")
    n_data = lax.axis_size("dp")
    devices_all = n_vocab * n_data
    capacity = max(4, 2 * tokens_here // devices_all)
    owner = token_ids // held_rows
    local_row = token_ids - owner * held_rows
    owner_hits = (owner[:, None] == jnp.arange(devices_all, dtype=jnp.int32)[None, :]).astype(
        jnp.int32
    )
    rank = jnp.sum(jnp.cumsum(owner_hits, axis=0) * owner_hits, axis=1) - 1
    slot_index = owner * capacity + rank
    requests = jnp.full((devices_all * capacity,), -1, jnp.int32).at[slot_index].set(local_row)
    received = move_ids(requests.reshape(devices_all, capacity)).reshape(-1)
    valid = received >= 0
    safe_rows = jnp.maximum(received, 0)
    picked = jnp.where(valid[:, None], table[safe_rows], jnp.zeros((1, width), table.dtype))
    returned = move_rows(picked.reshape(devices_all, capacity, width)).reshape(-1, width)
    embedded = returned[slot_index]
    live = jnp.arange(tokens_here, dtype=jnp.int32) < counts[0]
    product = jnp.dot(embedded, projection, preferred_element_type=jnp.float32)
    hidden = jnp.where(live[:, None], product, 0.0).astype(jnp.bfloat16)
    masked = jnp.where(live[:, None], cotangent, jnp.zeros_like(cotangent))
    token_grad = lax.dot_general(
        masked, projection, (((1,), (1,)), ((), ())), preferred_element_type=jnp.float32
    ).astype(jnp.bfloat16)
    outgoing = (
        jnp.zeros((devices_all * capacity, width), jnp.bfloat16).at[slot_index].set(token_grad)
    )
    incoming = move_rows(outgoing.reshape(devices_all, capacity, width)).reshape(-1, width)
    grad_table = jax.ops.segment_sum(
        incoming.astype(jnp.float32), safe_rows, num_segments=held_rows
    )
    terms = lax.dot_general(
        embedded, masked, (((0,), (0,)), ((), ())), preferred_element_type=jnp.float32
    )
    scaling = 1.0 / math.sqrt(tokens_here * devices_all)
    grad_projection = sum_projection(terms, scaling)
    return (hidden, grad_projection, grad_table)


def solution(mesh):
    return jax.shard_map(
        body,
        mesh=mesh,
        in_specs=(
            P(("vocab", "dp")),
            P(("vocab", "dp")),
            P(("vocab", "dp"), None),
            P(),
            P(("vocab", "dp"), None),
        ),
        out_specs=(P(("vocab", "dp"), None), P(), P(("vocab", "dp"), None)),
        check_vma=False,
    )
```

profile of v0, /device:TPU:1, one launch (start us, length us, event | category | flops | bytes accessed | tf_op | source)
XLA Modules:
  0.0 218.9 jit_solution(4850085707859522809)
XLA Ops:
  7.2 0.0 copy-start
  7.2 0.8 add_select_fusion
  8.0 9.0 %reduce-window.6 = s32[32,8,128]{2,1,0:T(8,128)S(1)} reduce-window(s32[32,8,128]{2,1,0:T(8,128)S(1)} %fusion.10, s32[]{:T(128)} %constant.15.clone.1), window={size=1x1x128 pad=0_0x0_0x127_0}, to_apply=%region_0.1 | reduce-window | flops 4161536 | bytes 262148 | tf_op jit(solution)/shard_map/reduce-window
  17.1 0.1 slice.12
  17.2 0.1 copy.12
  17.3 0.1 copy.13
  17.4 0.1 broadcast_add_fusion
  17.6 0.7 broadcast_clamp_fusion.1
  18.3 4.3 %scatter_custom_fusion = s32[2048]{0:T(1024)S(1)} fusion(s32[1024]{0:T(1024)S(1)} %get-tuple-element.4, s32[1024]{0:T(1024)S(1)} %get-tuple-element.5, s32[]{:T(128)} %constant.13.clone.1), kind=kCustom, calls=%fused_computation.35 | custom fusion | bytes 8196 | tf_op jit(solution)/shard_map/scatter | solution.py:36
  22.6 0.1 all_to_all.12
  22.7 13.6 %all_to_all.19 = s32[32,1,64]{2,1,0:T(1,128)S(1)} all-to-all(s32[32,1,64]{2,1,0:T(1,128)S(1)} %all_to_all.12), channel_id=1, replica_groups=mesh['vocab'=8,'dp'=4] {'vocab','dp'}, dimensions={0} | all-to-all | bytes 16384 | tf_op jit(solution)/shard_map/all_to_all | solution.py:10
  36.3 0.1 reshape.79
  36.4 0.0 copy-done
  36.4 6.2 %gather_fusion = bf16[2048,128]{1,0:T(8,128)(2,1)S(1)} fusion(bf16[8192,128]{1,0:T(8,128)(2,1)S(1)} %copy-done, s32[2048]{0:T(1024)S(1)} %broadcast_clamp_fusion), kind=kCustom, calls=%fused_computation | custom fusion | bytes 1056768 | tf_op jit(solution)/shard_map/gather | solution.py:40
  42.5 1.1 broadcast_select_fusion.5
  43.7 2.9 %all-to-all-start.1 = ((bf16[32,64,128]{2,1,0:T(8,128)(2,1)}), bf16[32,64,128]{2,1,0:T(8,128)(2,1)S(1)}, u32[]{:S(2)}, u32[]{:S(2)}) async-start(bf16[32,64,128]{2,1,0:T(8,128)(2,1)} %broadcast_select_fusion.5), calls=%async_computation.1 | async-start | bytes 1048576 | tf_op jit(solution)/shard_map/all_to_all | solution.py:14
  47.3 6.0 %fusion.4 = bf16[1024,128]{1,0:T(8,128)(2,1)S(1)} fusion(bf16[128,4096]{1,0:T(8,128)(2,1)} %param.8, bf16[1024,4096]{1,0:T(8,128)(2,1)} %param.9, pred[1024]{0:T(1024)(128)(4,1)S(1)} %iota_compare_fusion.2), kind=kOutput, calls=%fused_computation.11 | convolution fusion | flops 1078067200 | bytes 9700352 | tf_op jit(solution)/shard_map/dot_general | solution.py:47
  53.3 4.0 %scatter_custom_fusion.1 = bf16[2048,128]{1,0:T(8,128)(2,1)} fusion(s32[1024]{0:T(1024)S(1)} %get-tuple-element.4, bf16[1024,128]{1,0:T(8,128)(2,1)S(1)} %fusion.4, bf16[]{:T(256)} %constant.40.clone.1), kind=kCustom, calls=%fused_computation.15 | custom fusion | bytes 524290 | tf_op jit(solution)/shard_map/scatter | solution.py:51
  57.3 4.8 %all-to-all-done.1 = bf16[32,64,128]{2,1,0:T(8,128)(2,1)S(1)} async-done(((bf16[32,64,128]{2,1,0:T(8,128)(2,1)}), bf16[32,64,128]{2,1,0:T(8,128)(2,1)S(1)}, u32[]{:S(2)}, u32[]{:S(2)}) %all-to-all-start.1) | async-done | bytes 524320 | tf_op jit(solution)/shard_map/all_to_all | solution.py:14
  62.0 3.1 %all-to-all-start.2 = ((bf16[32,64,128]{2,1,0:T(8,128)(2,1)}), bf16[32,64,128]{2,1,0:T(8,128)(2,1)S(1)}, u32[]{:S(2)}, u32[]{:S(2)}) async-start(bf16[32,64,128]{2,1,0:T(8,128)(2,1)} %bitcast.38), calls=%async_computation.2 | async-start | bytes 1048576 | tf_op jit(solution)/shard_map/all_to_all | solution.py:14
  65.2 0.0 all-reduce.2.cloned.1.call-start
  65.2 3.2 %gather_fusion.1 = bf16[1024,128]{1,0:T(8,128)(2,1)S(1)} fusion(bf16[2048,128]{1,0:T(8,128)(2,1)S(1)} %bitcast.35, s32[1024]{0:T(1024)S(1)} %get-tuple-element.3), kind=kCustom, calls=%fused_computation.1 | custom fusion | bytes 528384 | tf_op jit(solution)/shard_map/gather | solution.py:42
  68.4 6.1 %fusion.1 = f32[128,4096]{1,0:T(8,128)} fusion(bf16[1024,128]{1,0:T(8,128)(2,1)S(1)} %gather_fusion.1, bf16[1024,4096]{1,0:T(8,128)(2,1)} %param.9, pred[1024]{0:T(1024)(128)(4,1)S(1)} %iota_compare_fusion.2), kind=kOutput, calls=%fused_computation.8 | convolution fusion | flops 1077936128 | bytes 10748928 | tf_op jit(solution)/shard_map/dot_general | solution.py:57
  74.5 0.0 all-reduce.2.cloned.1.call-update
  74.5 5.9 %all-to-all-done.2 = bf16[32,64,128]{2,1,0:T(8,128)(2,1)S(1)} async-done(((bf16[32,64,128]{2,1,0:T(8,128)(2,1)}), bf16[32,64,128]{2,1,0:T(8,128)(2,1)S(1)}, u32[]{:S(2)}, u32[]{:S(2)}) %all-to-all-start.2) | async-done | bytes 524320 | tf_op jit(solution)/shard_map/all_to_all | solution.py:14
  80.4 13.9 %scatter_custom_fusion.2 = f32[8192,128]{1,0:T(8,128)} fusion(s32[2048]{0:T(1024)S(1)} %reshape.79, f32[]{:T(128)} %constant.41.clone.1, bf16[2048,128]{1,0:T(8,128)(2,1)S(1)} %bitcast.36), kind=kCustom, calls=%fused_computation.9 | custom fusion | flops 524288 | bytes 4718596 | tf_op jit(solution)/shard_map/scatter-add | solution.py:54
  94.3 5.9 %select_convert_fusion = bf16[1024,4096]{1,0:T(8,128)(2,1)} fusion(bf16[1024,128]{1,0:T(8,128)(2,1)S(1)} %gather_fusion.1, bf16[128,4096]{1,0:T(8,128)(2,1)} %param.8, pred[1024]{0:T(1024)(128)(4,1)S(1)} %iota_compare_fusion.2), kind=kOutput, calls=%fused_computation.5 | convolution fusion | flops 1082130432 | bytes 9700352 | tf_op jit(solution)/shard_map/dot_general | solution.py:44
  100.2 108.7 %all-reduce.2.cloned.1.call-done = f32[128,4096]{1,0:T(8,128)} async-done(((f32[128,4096]{1,0:T(8,128)}), f32[128,4096]{1,0:T(8,128)}) %all-reduce.2.cloned.1.call-update) | async-done | bytes 2097168 | tf_op jit(solution)/shard_map/psum | solution.py:18
  208.9 3.1 %broadcast_multiply_fusion = f32[128,4096]{1,0:T(8,128)} fusion(f32[128,4096]{1,0:T(8,128)} %all-reduce.2.cloned.1.call-done), kind=kLoop, calls=%fused_computation.13 | loop fusion | flops 524288 | bytes 4194304 | tf_op jit(solution)/shard_map/mul | solution.py:18
  (8 shorter events, 0.1 us)
Async XLA Ops:
  7.2 29.2 %copy-start = (bf16[8192,128]{1,0:T(8,128)(2,1)S(1)}, bf16[8192,128]{1,0:T(8,128)(2,1)}, u32[]{:S(2)}) copy-start(bf16[8192,128]{1,0:T(8,128)(2,1)} %param.7) | copy-start | bytes 6291460
  43.7 18.4 %all-to-all-start.1 = ((bf16[32,64,128]{2,1,0:T(8,128)(2,1)}), bf16[32,64,128]{2,1,0:T(8,128)(2,1)S(1)}, u32[]{:S(2)}, u32[]{:S(2)}) async-start(bf16[32,64,128]{2,1,0:T(8,128)(2,1)} %broadcast_select_fusion.5), calls=%async_computation.1 | async-start | bytes 1048576 | tf_op jit(solution)/shard_map/all_to_all | solution.py:14
  62.0 18.4 %all-to-all-start.2 = ((bf16[32,64,128]{2,1,0:T(8,128)(2,1)}), bf16[32,64,128]{2,1,0:T(8,128)(2,1)S(1)}, u32[]{:S(2)}, u32[]{:S(2)}) async-start(bf16[32,64,128]{2,1,0:T(8,128)(2,1)} %bitcast.38), calls=%async_computation.2 | async-start | bytes 1048576 | tf_op jit(solution)/shard_map/all_to_all | solution.py:14
  65.2 143.7 %all-reduce.2.cloned.1.call-start = ((), (), s32[]{:S(2)}) async-start(), calls=%async_computation.3 | async-start | bytes 4194304 | tf_op jit(solution)/shard_map/psum | solution.py:18
Sparse Core Ops, SparseCore 0:
  74.6 134.1 all-reduce.1
where the time goes:
time: 221 us; the launch traced here: 219 us
  waiting for transfers between devices  119 us (54%)
  other arithmetic  28.9 us (13%)
  local copies, waits for them, and re-layouts  18.1 us (8%)
  matrix products  17.9 us (8%)
  between operations  14.8 us (7%)
  blocking collectives  13.6 us (6%)
  starting transfers between devices  6.11 us (3%)
    psum x1, waiting for transfers between devices, sum_projection(): return lax.psum(terms, ('vocab', 'dp')) * scaling  109 us
    scatter-add x1, other arithmetic, body(): jax.ops.segment_sum(incoming.astype(jnp.float32), safe_rows, num_segments...  13.9 us
    all_to_all x1, blocking collectives, move_ids(): lax.all_to_all(requests, ('vocab', 'dp'), split_axis=0, concat_axis=0, ti...  13.6 us
    all_to_all x2, waiting for transfers between devices, move_rows(): lax.all_to_all(blocks, ('vocab', 'dp'), split_axis=0, concat_axis=0, tile...  10.7 us
    another operation x3, other arithmetic  9.15 us
    gather x1, local copies, waits for them, and re-layouts, body(): table[safe_rows]  6.18 us
    all_to_all x2, starting transfers between devices, move_rows(): lax.all_to_all(blocks, ('vocab', 'dp'), split_axis=0, concat_axis=0, tile...  6.07 us
    dot_general x1, matrix products, body(): lax.dot_general(embedded, masked, (((0,), (0,)), ((), ())), preferred_ele...  6.06 us
  transfers between devices with their start and end apart: 3, of which 3 were waited for; matrix products, arithmetic and copies ran while one was open for 18% of the time, Pallas kernels for 0%

commit v1 on v0

v1 whole, which is shorter than its diff:
```python
import functools
import math

import jax
import jax.numpy as jnp
from jax import lax
from jax.experimental import pallas as pl
from jax.experimental.pallas import tpu as pltpu
from jax.sharding import PartitionSpec as P

AXES = ("vocab", "dp")
ACCS = 4


def exchange(blocks):
    return lax.all_to_all(blocks, AXES, split_axis=0, concat_axis=0, tiled=True)


def scatter_kernel(chunks, rows_ref, incoming_ref, out_ref, acc0, acc1, acc2, acc3, sems):
    accs = (acc0, acc1, acc2, acc3)
    held = acc0.shape[0]
    part = held // chunks
    count = incoming_ref.shape[0]

    def clear(i, carry):
        at = pl.ds(pl.multiple_of(i * 64, 64), 64)
        for acc in accs:
            acc[at, :] = jnp.zeros((64, acc.shape[1]), jnp.float32)
        return carry

    lax.fori_loop(0, held // 64, clear, 0)

    def add(i, carry):
        base = pl.multiple_of(i * 8, 8)
        block = incoming_ref[pl.ds(base, 8), :]
        for j in range(8):
            acc = accs[j % ACCS]
            at = pl.ds(rows_ref[base + j], 1)
            acc[at, :] = acc[at, :] + block[j : j + 1, :]
        return carry

    lax.fori_loop(0, count // 8, add, 0)

    def copy(c):
        at = pl.ds(c * part, part)
        return pltpu.make_async_copy(acc0.at[at, :], out_ref.at[at, :], sems.at[c])

    for c in range(chunks):

        def join(i, carry):
            at = pl.ds(pl.multiple_of(c * part + i * 64, 64), 64)
            acc0[at, :] = (acc0[at, :] + acc1[at, :]) + (acc2[at, :] + acc3[at, :])
            return carry

        lax.fori_loop(0, part // 64, join, 0)
        copy(c).start()
    for c in range(chunks):
        copy(c).wait()


def scatter_rows(rows, incoming, held_rows):
    width = incoming.shape[1]
    chunks = 4
    return pl.pallas_call(
        functools.partial(scatter_kernel, chunks),
        out_shape=jax.ShapeDtypeStruct((held_rows, width), jnp.float32),
        in_specs=[
            pl.BlockSpec(memory_space=pltpu.SMEM),
            pl.BlockSpec(memory_space=pltpu.VMEM),
        ],
        out_specs=pl.BlockSpec(memory_space=pl.ANY),
        scratch_shapes=[pltpu.VMEM((held_rows, width), jnp.float32)] * ACCS
        + [pltpu.SemaphoreType.DMA((chunks,))],
        cost_estimate=pl.CostEstimate(flops=0, bytes_accessed=12 << 20, transcendentals=0),
        name="scatter_rows",
    )(rows, incoming)


def body(token_ids, counts, table, projection, cotangent):
    tokens_here = token_ids.shape[0]
    held_rows = table.shape[0]
    width = table.shape[1]
    hidden_width = projection.shape[1]
    devices_all = lax.axis_size("vocab") * lax.axis_size("dp")
    capacity = max(4, 2 * tokens_here // devices_all)
    slots = devices_all * capacity
    bf16, f32 = jnp.bfloat16, jnp.float32

    owner = token_ids // held_rows
    local_row = token_ids - owner * held_rows
    hits = (owner[:, None] == jnp.arange(devices_all, dtype=jnp.int32)[None, :]).astype(bf16)
    order = jnp.arange(tokens_here, dtype=jnp.int32)
    before = (order[:, None] >= order[None, :]).astype(bf16)
    ranks = jnp.dot(before, hits, preferred_element_type=f32)
    rank = jnp.sum(ranks * hits.astype(f32), axis=1).astype(jnp.int32) - 1
    slot_index = owner * capacity + rank
    place = (slot_index[:, None] == jnp.arange(slots, dtype=jnp.int32)[None, :]).astype(bf16)
    digits = jnp.stack(
        [local_row // 65536, (local_row // 256) % 256, local_row % 256, jnp.ones_like(local_row)]
    ).astype(bf16)
    found = jnp.dot(digits, place, preferred_element_type=f32).astype(jnp.int32)
    requests = found[0] * 65536 + found[1] * 256 + found[2] + found[3] - 1
    requests = jnp.where(found[3] > 0, requests, -1)

    received = exchange(requests.reshape(devices_all, capacity)).reshape(-1)
    valid = received >= 0
    safe_rows = jnp.maximum(received, 0)
    picked = jnp.where(valid[:, None], table[safe_rows], jnp.zeros((1, width), table.dtype))
    returned = exchange(picked.reshape(devices_all, capacity, width)).reshape(-1, width)

    live = order < counts[0]
    masked = jnp.where(live[:, None], cotangent, jnp.zeros_like(cotangent))
    token_grad = lax.dot_general(
        masked, projection, (((1,), (1,)), ((), ())), preferred_element_type=f32
    ).astype(bf16)
    outgoing = lax.dot_general(
        place, token_grad, (((0,), (0,)), ((), ())), preferred_element_type=f32
    ).astype(bf16)
    incoming = exchange(outgoing.reshape(devices_all, capacity, width)).reshape(-1, width)

    embedded = jnp.dot(place, returned, preferred_element_type=f32).astype(bf16)
    terms = lax.dot_general(
        masked, embedded, (((0,), (0,)), ((), ())), preferred_element_type=f32
    ).astype(bf16)
    share = hidden_width // devices_all
    parts = exchange(terms.reshape(devices_all, share, width))
    scaling = 1.0 / math.sqrt(tokens_here * devices_all)
    summed = (jnp.sum(parts.astype(f32), axis=0) * scaling).astype(bf16)
    spread = exchange(jnp.broadcast_to(summed[None], (devices_all, share, width)))
    grad_projection = spread.reshape(hidden_width, width).T.astype(f32)

    product = jnp.dot(embedded, projection, preferred_element_type=f32)
    hidden = jnp.where(live[:, None], product, 0.0).astype(bf16)
    grad_table = scatter_rows(safe_rows, incoming.astype(f32), held_rows)
    return (hidden, grad_projection, grad_table)


def solution(mesh):
    return jax.shard_map(
        body,
        mesh=mesh,
        in_specs=(
            P(AXES),
            P(AXES),
            P(AXES, None),
            P(),
            P(AXES, None),
        ),
        out_specs=(P(AXES, None), P(), P(AXES, None)),
        check_vma=False,
    )
```

time: 221 us -> 138 us (0.62)
  waiting for transfers between devices: 119 us -> 57.5 us
  other arithmetic: 28.9 us -> 6.55 us
  between operations: 14.8 us -> 1.45 us
  Pallas kernels: 0 us -> 8.85 us
  matrix products: 17.9 us -> 24.9 us
  starting transfers between devices: 6.11 us -> 12.5 us
  local copies, waits for them, and re-layouts: 18.1 us -> 12.2 us
    psum x1 -> x0, waiting for transfers between devices: 109 us -> none  [sum_projection(): return lax.psum(terms, ('vocab', 'dp')) * scaling]
    all_to_all x2 -> x4, waiting for transfers between devices: 10.7 us -> 57.5 us  [exchange(): return lax.all_to_all(blocks, AXES, split_axis=0, concat_axis=0, tiled=True)]
    scatter-add x1 -> x0, other arithmetic: 13.9 us -> none  [body(): jax.ops.segment_sum(incoming.astype(jnp.float32), safe_rows, num_segments...]
    pallas_call x0 -> x1, Pallas kernels: none -> 8.85 us  [scatter_rows(): pl.pallas_call(functools.partial(scatter_kernel, chunks), out_shape=jax.S...]
    another operation x3 -> x1, other arithmetic: 9.15 us -> 0.72 us
    scatter x2 -> x0, local copies, waits for them, and re-layouts: 8.3 us -> none  [the longest x1 4.32 us: body(): jnp.full((devices_all * capacity,), -1, jnp.int32).at[slot_index]]
    dot_general x2 -> x6, matrix products: 12 us -> 18.9 us  [the longest x1 7.29 us: body(): lax.dot_general(masked, embedded, (((0,), (0,)), ((), ())), preferred_ele...]
    all_to_all x2 -> x4, starting transfers between devices: 6.07 us -> 12.5 us  [exchange(): return lax.all_to_all(blocks, AXES, split_axis=0, concat_axis=0, tiled=True)]
  transfers between devices with their start and end apart: 3 -> 4, of which waited for: 3 -> 4; matrix products, arithmetic and copies ran while one was open for 18% -> 12% of each run, Pallas kernels for 0% -> 6%
where the time goes in v1:
time: 138 us
  waiting for transfers between devices  57.5 us (42%)
  matrix products  24.9 us (18%)
  blocking collectives  13.6 us (10%)
  starting transfers between devices  12.5 us (9%)
  local copies, waits for them, and re-layouts  12.2 us (9%)
  Pallas kernels  8.85 us (6%)
  other arithmetic  6.55 us (5%)
  between operations  1.45 us (1%)
    all_to_all x4, waiting for transfers between devices, exchange(): return lax.all_to_all(blocks, AXES, split_axis=0, concat_axis=0, tiled=True)  57.5 us
    all_to_all x1, blocking collectives, exchange(): return lax.all_to_all(blocks, AXES, split_axis=0, concat_axis=0, tiled=True)  13.6 us
    all_to_all x4, starting transfers between devices, exchange(): return lax.all_to_all(blocks, AXES, split_axis=0, concat_axis=0, tiled=True)  12.5 us
    pallas_call x1, Pallas kernels, scatter_rows(): pl.pallas_call(functools.partial(scatter_kernel, chunks), out_shape=jax.S...  8.85 us
    dot_general x1, matrix products, body(): lax.dot_general(masked, embedded, (((0,), (0,)), ((), ())), preferred_ele...  7.29 us
    gather x1, local copies, waits for them, and re-layouts, body(): table[safe_rows]  6.18 us
    dot_general x1, matrix products, body(): lax.dot_general(masked, projection, (((1,), (1,)), ((), ())), preferred_e...  5.98 us
    dot_general x1, matrix products, body(): product = jnp.dot(embedded, projection, preferred_element_type=f32)  4.67 us
  transfers between devices with their start and end apart: 4, of which 4 were waited for; matrix products, arithmetic and copies ran while one was open for 12% of the time, Pallas kernels for 6%

profile of v1, /device:TPU:1, one launch (start us, length us, event | category | flops | bytes accessed | tf_op | source)
XLA Modules:
  0.0 137.6 jit_solution(5817402854901861591)
XLA Ops:
  0.6 0.8 add_select_fusion.4
  1.5 0.5 fusion.13
  2.0 0.7 fusion.28
  2.8 0.1 pad.3.clone
  2.9 1.6 %fusion.9 = s32[4,2048]{1,0:T(4,128)S(1)} fusion(s32[1024]{0:T(1024)S(1)} %get-tuple-element.7, bf16[1,1024]{1,0:T(2,128)(2,1)S(1)} %stack.18, bf16[1,1024]{1,0:T(2,128)(2,1)S(1)} %stack.17, bf16[1,1024]{1,0:T(2,128)(2,1)S(1)} %stack.16, bf16[4]{0:T(256)(128)(2,1)S(1)} %pad.3.clone), kind=kOutput, calls=%fused_computation.15 | convolution fusion | flops 18915328 | bytes 43016 | tf_op jit(solution)/shard_map/dot_general | solution.py:101
  4.5 0.1 fusion.16
  4.5 0.1 reshape.147
  4.6 13.6 %all_to_all.26 = s32[32,1,64]{2,1,0:T(1,128)S(1)} all-to-all(s32[32,1,64]{2,1,0:T(1,128)S(1)} %bitcast.34), channel_id=1, replica_groups=mesh['vocab'=8,'dp'=4] {'vocab','dp'}, dimensions={0} | all-to-all | bytes 16384 | tf_op jit(solution)/shard_map/all_to_all | solution.py:16
  18.2 0.1 reshape.151.rows_ref
  18.3 6.2 %gather_fusion = bf16[2048,128]{1,0:T(8,128)(2,1)S(1)} fusion(bf16[8192,128]{1,0:T(8,128)(2,1)S(1)} %copy-done, s32[2048]{0:T(1024)S(1)} %broadcast_clamp_fusion), kind=kCustom, calls=%fused_computation | custom fusion | bytes 1056768 | tf_op jit(solution)/shard_map/gather | solution.py:108
  24.5 1.1 broadcast_select_fusion.5
  25.6 3.0 %all-to-all-start.1 = ((bf16[32,64,128]{2,1,0:T(8,128)(2,1)}), bf16[32,64,128]{2,1,0:T(8,128)(2,1)S(1)}, u32[]{:S(2)}, u32[]{:S(2)}) async-start(bf16[32,64,128]{2,1,0:T(8,128)(2,1)} %broadcast_select_fusion.5), calls=%async_computation.1 | async-start | bytes 1048576 | tf_op jit(solution)/shard_map/all_to_all | solution.py:16
  29.2 14.7 %all-to-all-done.1 = bf16[32,64,128]{2,1,0:T(8,128)(2,1)S(1)} async-done(((bf16[32,64,128]{2,1,0:T(8,128)(2,1)}), bf16[32,64,128]{2,1,0:T(8,128)(2,1)S(1)}, u32[]{:S(2)}, u32[]{:S(2)}) %all-to-all-start.1) | async-done | bytes 524320 | tf_op jit(solution)/shard_map/all_to_all | solution.py:16
  44.0 1.5 %fusion.11 = bf16[1024,128]{1,0:T(8,128)(2,1)S(1)} fusion(bf16[2048,128]{1,0:T(8,128)(2,1)S(1)} %bitcast.31, s32[1024]{0:T(1024)S(1)} %get-tuple-element.7), kind=kOutput, calls=%fused_computation.19 | convolution fusion | flops 539099136 | bytes 790528 | tf_op jit(solution)/shard_map/dot_general | solution.py:121
  45.5 7.3 %convolution_convert_fusion = bf16[4096,128]{1,0:T(8,128)(2,1)} fusion(bf16[1024,128]{1,0:T(8,128)(2,1)S(1)} %fusion.11, bf16[1024,4096]{1,0:T(8,128)(2,1)} %param.9, pred[1024]{0:T(1024)(128)(4,1)S(1)} %iota_compare_fusion.18), kind=kOutput, calls=%fused_computation.7 | convolution fusion | flops 1078460416 | bytes 9700352 | tf_op jit(solution)/shard_map/dot_general | solution.py:122
  52.8 3.1 %all-to-all-start.2 = ((bf16[32,128,128]{2,1,0:T(8,128)(2,1)}), bf16[32,128,128]{2,1,0:T(8,128)(2,1)S(1)}, u32[]{:S(2)}, u32[]{:S(2)}) async-start(bf16[32,128,128]{2,1,0:T(8,128)(2,1)} %bitcast.29), calls=%async_computation.2 | async-start | bytes 2097152 | tf_op jit(solution)/shard_map/all_to_all | solution.py:16
  55.9 6.0 %fusion.10 = bf16[1024,128]{1,0:T(8,128)(2,1)S(1)} fusion(bf16[128,4096]{1,0:T(8,128)(2,1)} %param.8, bf16[1024,4096]{1,0:T(8,128)(2,1)} %param.9, pred[1024]{0:T(1024)(128)(4,1)S(1)} %iota_compare_fusion.18), kind=kOutput, calls=%fused_computation.18 | convolution fusion | flops 1078067200 | bytes 9700352 | tf_op jit(solution)/shard_map/dot_general | solution.py:113
  61.9 3.3 %fusion.8 = bf16[2048,128]{1,0:T(8,128)(2,1)} fusion(bf16[1024,128]{1,0:T(8,128)(2,1)S(1)} %fusion.10, s32[1024]{0:T(1024)S(1)} %get-tuple-element.7), kind=kOutput, calls=%fused_computation.14 | convolution fusion | flops 539230208 | bytes 790528 | tf_op jit(solution)/shard_map/dot_general | solution.py:116
  65.2 17.0 %all-to-all-done.2 = bf16[32,128,128]{2,1,0:T(8,128)(2,1)S(1)} async-done(((bf16[32,128,128]{2,1,0:T(8,128)(2,1)}), bf16[32,128,128]{2,1,0:T(8,128)(2,1)S(1)}, u32[]{:S(2)}, u32[]{:S(2)}) %all-to-all-start.2) | async-done | bytes 1048608 | tf_op jit(solution)/shard_map/all_to_all | solution.py:16
  82.2 3.2 %all-to-all-start.4 = ((bf16[32,64,128]{2,1,0:T(8,128)(2,1)}), bf16[32,64,128]{2,1,0:T(8,128)(2,1)}, u32[]{:S(2)}, u32[]{:S(2)}) async-start(bf16[32,64,128]{2,1,0:T(8,128)(2,1)} %bitcast.30), calls=%async_computation.4 | async-start | bytes 1048576 | tf_op jit(solution)/shard_map/all_to_all | solution.py:16
  85.4 0.2 convert_reduce_fusion
  85.6 0.1 copy.13
  85.7 15.0 %all-to-all-done.4 = bf16[32,64,128]{2,1,0:T(8,128)(2,1)} async-done(((bf16[32,64,128]{2,1,0:T(8,128)(2,1)}), bf16[32,64,128]{2,1,0:T(8,128)(2,1)}, u32[]{:S(2)}, u32[]{:S(2)}) %all-to-all-start.4) | async-done | bytes 524320 | tf_op jit(solution)/shard_map/all_to_all | solution.py:16
  100.7 1.2 broadcast_in_dim.61
  102.0 3.2 %all-to-all-start.3 = ((bf16[32,128,128]{1,2,0:T(8,128)(2,1)}), bf16[32,128,128]{1,2,0:T(8,128)(2,1)}, u32[]{:S(2)}, u32[]{:S(2)}) async-start(bf16[32,128,128]{1,2,0:T(8,128)(2,1)} %broadcast_in_dim.61), calls=%async_computation.3 | async-start | bytes 2097152 | tf_op jit(solution)/shard_map/all_to_all | solution.py:16
  105.2 2.1 %bitcast_convert_fusion.incoming_ref = f32[2048,128]{1,0:T(8,128)} fusion(bf16[32,64,128]{2,1,0:T(8,128)(2,1)} %all-to-all-done.4), kind=kLoop, calls=%fused_computation.22 | loop fusion | flops 262144 | bytes 1572864 | tf_op jit(solution)/shard_map/convert_element_type | solution.py:134
  107.2 8.8 %scatter_rows.1 = f32[8192,128]{1,0:T(8,128)} custom-call(s32[2048]{0:T(1024)} %copy-done.1, f32[2048,128]{1,0:T(8,128)} %bitcast_convert_fusion.incoming_ref), custom_call_target="tpu_custom_call" | custom-call | bytes 12582912 | tf_op jit(solution)/shard_map/scatter_rows/pallas_call | solution.py:64
  116.1 4.7 %select_convert_fusion = bf16[1024,4096]{1,0:T(8,128)(2,1)} fusion(bf16[1024,128]{1,0:T(8,128)(2,1)S(1)} %fusion.11, bf16[128,4096]{1,0:T(8,128)(2,1)S(1)} %copy-done.2, pred[1024]{0:T(1024)(128)(4,1)S(1)} %iota_compare_fusion.18), kind=kOutput, calls=%fused_computation.1 | convolution fusion | flops 1082130432 | bytes 9700352 | tf_op jit(solution)/shard_map/dot_general | solution.py:132
  120.8 10.8 %all-to-all-done.3 = bf16[32,128,128]{1,2,0:T(8,128)(2,1)} async-done(((bf16[32,128,128]{1,2,0:T(8,128)(2,1)}), bf16[32,128,128]{1,2,0:T(8,128)(2,1)}, u32[]{:S(2)}, u32[]{:S(2)}) %all-to-all-start.3) | async-done | bytes 1048608 | tf_op jit(solution)/shard_map/all_to_all | solution.py:16
  131.5 1.6 %copy.14 = bf16[32,128,128]{2,1,0:T(8,128)(2,1)S(1)} copy(bf16[32,128,128]{1,2,0:T(8,128)(2,1)} %all-to-all-done.3) | data formatting | bytes 2097152 | tf_op jit(solution)/shard_map/all_to_all | solution.py:16
  133.2 1.5 %convert_bitcast_fusion = f32[128,4096]{0,1:T(8,128)} fusion(bf16[32,128,128]{2,1,0:T(8,128)(2,1)S(1)} %copy.14), kind=kLoop, calls=%fused_computation.16 | loop fusion | flops 524288 | bytes 3145728 | tf_op jit(solution)/shard_map/convert_element_type | solution.py:130
  134.7 2.9 %copy.15 = f32[128,4096]{1,0:T(8,128)} copy(f32[128,4096]{0,1:T(8,128)} %convert_bitcast_fusion) | data formatting | bytes 4194304
  (14 shorter events, 0.1 us)
Async XLA Ops:
  0.6 17.7 %copy-start = (bf16[8192,128]{1,0:T(8,128)(2,1)S(1)}, bf16[8192,128]{1,0:T(8,128)(2,1)}, u32[]{:S(2)}) copy-start(bf16[8192,128]{1,0:T(8,128)(2,1)} %param.7) | copy-start | bytes 6291460
  18.3 34.5 %copy-start.1 = (s32[2048]{0:T(1024)}, s32[2048]{0:T(1024)S(1)}, u32[]{:S(2)}) copy-start(s32[2048]{0:T(1024)S(1)} %reshape.151.rows_ref) | copy-start | bytes 24580
  25.6 18.4 %all-to-all-start.1 = ((bf16[32,64,128]{2,1,0:T(8,128)(2,1)}), bf16[32,64,128]{2,1,0:T(8,128)(2,1)S(1)}, u32[]{:S(2)}, u32[]{:S(2)}) async-start(bf16[32,64,128]{2,1,0:T(8,128)(2,1)} %broadcast_select_fusion.5), calls=%async_computation.1 | async-start | bytes 1048576 | tf_op jit(solution)/shard_map/all_to_all | solution.py:16
  52.8 29.5 %all-to-all-start.2 = ((bf16[32,128,128]{2,1,0:T(8,128)(2,1)}), bf16[32,128,128]{2,1,0:T(8,128)(2,1)S(1)}, u32[]{:S(2)}, u32[]{:S(2)}) async-start(bf16[32,128,128]{2,1,0:T(8,128)(2,1)} %bitcast.29), calls=%async_computation.2 | async-start | bytes 2097152 | tf_op jit(solution)/shard_map/all_to_all | solution.py:16
  82.2 18.5 %all-to-all-start.4 = ((bf16[32,64,128]{2,1,0:T(8,128)(2,1)}), bf16[32,64,128]{2,1,0:T(8,128)(2,1)}, u32[]{:S(2)}, u32[]{:S(2)}) async-start(bf16[32,64,128]{2,1,0:T(8,128)(2,1)} %bitcast.30), calls=%async_computation.4 | async-start | bytes 1048576 | tf_op jit(solution)/shard_map/all_to_all | solution.py:16
  85.6 30.5 %copy-start.2 = (bf16[128,4096]{1,0:T(8,128)(2,1)S(1)}, bf16[128,4096]{1,0:T(8,128)(2,1)}, u32[]{:S(2)}) copy-start(bf16[128,4096]{1,0:T(8,128)(2,1)} %param.8) | copy-start | bytes 3145732
  102.0 29.6 %all-to-all-start.3 = ((bf16[32,128,128]{1,2,0:T(8,128)(2,1)}), bf16[32,128,128]{1,2,0:T(8,128)(2,1)}, u32[]{:S(2)}, u32[]{:S(2)}) async-start(bf16[32,128,128]{1,2,0:T(8,128)(2,1)} %broadcast_in_dim.61), calls=%async_computation.3 | async-start | bytes 2097152 | tf_op jit(solution)/shard_map/all_to_all | solution.py:16

commit v2 on v1

--- a/solution.py
+++ b/solution.py
@@ -75,6 +75,208 @@
         name="scatter_rows",
     )(rows, incoming)
 
+MESH = pl.DeviceIdType.MESH
+LANES = 128
+
+
+def remote(src, dst, send_sem, recv_sem, where):
+    return pltpu.make_async_remote_copy(
+        src_ref=src, dst_ref=dst, send_sem=send_sem, recv_sem=recv_sem,
+        device_id=where, device_id_type=MESH,
+    )
+
+
+def reduce_kernel(
+    n_vocab, n_dp, split, scaling, emb_ref, cot_ref, out_ref,
+    cot_buf, emb_t, send_a, recv_a, acc_a, send_b, recv_b, acc_b, recv_c, full,
+    load_sem, sa, ra, sb, rb, sc, rc, sd, rd, se, re, sf, rf,
+):
+    f32, bf16 = jnp.float32, jnp.bfloat16
+    v = lax.axis_index("vocab")
+    z = lax.axis_index("dp")
+    core, chip = lax.rem(v, 2), v // 2
+    chips = n_vocab // 2
+    width, hidden_width = out_ref.shape
+    half = hidden_width // 2
+    span = half // split
+    rows_a = width * span // LANES
+    rows_b = rows_a // chips
+    rows_c = rows_b // n_dp
+    tile = min(256, span)
+    partner = (chip * 2 + 1 - core, z)
+
+    def in_plane(k):
+        return (lax.rem(chip + k, chips) * 2 + core, z)
+
+    def in_line(k):
+        return (v, lax.rem(z + k, n_dp))
+
+    def load(j):
+        side = (1 - core) if j < split else core
+        at = pl.ds(pl.multiple_of(side * half + (j % split) * span, LANES), span)
+        return pltpu.make_async_copy(cot_ref.at[:, at], cot_buf.at[j], load_sem.at[j])
+
+    for j in range(2 * split):
+        load(j).start()
+    barrier = pltpu.get_barrier_semaphore()
+    peers = [partner] + [in_plane(k) for k in range(1, chips)] + [in_line(k) for k in range(1, n_dp)]
+    for where in peers:
+        pl.semaphore_signal(barrier, inc=1, device_id=where, device_id_type=MESH)
+    emb_t[...] = emb_ref[...].T
+
+    def product(j, target):
+        def step(t, carry):
+            at = pl.ds(pl.multiple_of(t * tile, tile), tile)
+            y = jnp.dot(emb_t[...], cot_buf[j, :, at], preferred_element_type=f32)
+            for b in range(tile // LANES):
+                rows = pl.ds(pl.multiple_of((t * (tile // LANES) + b) * width, width), width)
+                target[rows, :] = y[:, b * LANES : (b + 1) * LANES].astype(target.dtype)
+            return carry
+
+        lax.fori_loop(0, span // tile, step, 0)
+
+    def copy_a(q):
+        return remote(send_a.at[q], recv_a.at[q], sa.at[q], ra.at[q], partner)
+
+    def copy_b(q, k):
+        to = lax.rem(chip + k, chips)
+        rows = pl.ds(pl.multiple_of(to * rows_b, rows_b), rows_b)
+        return remote(
+            send_b.at[q, rows, :], recv_b.at[q, k - 1], sb.at[q, k - 1], rb.at[q, k - 1], in_plane(k)
+        )
+
+    def copy_c(q, k):
+        to = lax.rem(z + k, n_dp)
+        rows = pl.ds(pl.multiple_of(to * rows_c, rows_c), rows_c)
+        return remote(
+            acc_b.at[q, rows, :], recv_c.at[q, k - 1], sc.at[q, k - 1], rc.at[q, k - 1], in_line(k)
+        )
+
+    def copy_d(q, k):
+        rows = pl.ds(pl.multiple_of(chip * rows_b + z * rows_c, rows_c), rows_c)
+        piece = full.at[core, q, rows, :]
+        return remote(piece, piece, sd.at[q, k - 1], rd.at[q, k - 1], in_line(k))
+
+    def copy_e(q, k):
+        rows = pl.ds(pl.multiple_of(chip * rows_b, rows_b), rows_b)
+        piece = full.at[core, q, rows, :]
+        return remote(piece, piece, se.at[q, k - 1], re.at[q, k - 1], in_plane(k))
+
+    def copy_f(q):
+        piece = full.at[core, q]
+        return remote(piece, piece, sf.at[q], rf.at[q], partner)
+
+    for q in range(split):
+        load(q).wait()
+        product(q, send_a.at[q])
+        if q == 0:
+            pl.semaphore_wait(barrier, len(peers))
+        copy_a(q).start()
+    for q in range(split):
+        load(split + q).wait()
+        product(split + q, acc_a.at[q])
+    plane = range(1, chips)
+    line = range(1, n_dp)
+    for q in range(split):
+        copy_a(q).wait_recv()
+        acc_a[q] = acc_a[q] + recv_a[q].astype(f32)
+        send_b[q] = acc_a[q].astype(bf16)
+        for k in plane:
+            copy_b(q, k).start()
+    for q in range(split):
+        own = pl.ds(pl.multiple_of(chip * rows_b, rows_b), rows_b)
+        total = acc_a[q, own, :]
+        for k in plane:
+            copy_b(q, k).wait_recv()
+            total = total + recv_b[q, k - 1].astype(f32)
+        acc_b[q] = total
+        for k in line:
+            copy_c(q, k).start()
+    for q in range(split):
+        own = pl.ds(pl.multiple_of(z * rows_c, rows_c), rows_c)
+        total = acc_b[q, own, :]
+        for k in line:
+            copy_c(q, k).wait_recv()
+            total = total + recv_c[q, k - 1]
+        rows = pl.ds(pl.multiple_of(chip * rows_b + z * rows_c, rows_c), rows_c)
+        full[core, q, rows, :] = (total * scaling).astype(bf16)
+        for k in line:
+            copy_d(q, k).start()
+    for q in range(split):
+        for k in line:
+            copy_d(q, k).wait_recv()
+        for k in plane:
+            copy_e(q, k).start()
+    for q in range(split):
+        for k in plane:
+            copy_e(q, k).wait_recv()
+        copy_f(q).start()
+
+    def unpack(side, q):
+        for b in range(span // LANES):
+            at = pl.ds(pl.multiple_of(side * half + q * span + b * LANES, LANES), LANES)
+            out_ref[:, at] = full[side, q, pl.ds(b * width, width), :]
+
+    for q in range(split):
+        unpack(core, q)
+    for q in range(split):
+        copy_f(q).wait_recv()
+        unpack(1 - core, q)
+    for q in range(split):
+        copy_a(q).wait_send()
+        copy_f(q).wait_send()
+        for k in plane:
+            copy_b(q, k).wait_send()
+            copy_e(q, k).wait_send()
+        for k in line:
+            copy_c(q, k).wait_send()
+            copy_d(q, k).wait_send()
+
+
+def reduce_terms(embedded, cotangent, scaling):
+    n_vocab, n_dp = lax.axis_size("vocab"), lax.axis_size("dp")
+    tokens, width = embedded.shape
+    hidden_width = cotangent.shape[1]
+    split = 2
+    chips = n_vocab // 2
+    span = hidden_width // (2 * split)
+    rows_a = width * span // LANES
+    rows_b = rows_a // chips
+    rows_c = rows_b // n_dp
+    f32, bf16 = jnp.float32, jnp.bfloat16
+    dma = pltpu.SemaphoreType.DMA
+    plane, line = max(1, chips - 1), max(1, n_dp - 1)
+    return pl.pallas_call(
+        functools.partial(reduce_kernel, n_vocab, n_dp, split, scaling),
+        out_shape=jax.ShapeDtypeStruct((width, hidden_width), bf16),
+        in_specs=[
+            pl.BlockSpec(memory_space=pltpu.VMEM),
+            pl.BlockSpec(memory_space=pl.ANY),
+        ],
+        out_specs=pl.BlockSpec(memory_space=pltpu.VMEM),
+        scratch_shapes=[
+            pltpu.VMEM((2 * split, tokens, span), bf16),
+            pltpu.VMEM((width, tokens), bf16),
+            pltpu.VMEM((split, rows_a, LANES), bf16),
+            pltpu.VMEM((split, rows_a, LANES), bf16),
+            pltpu.VMEM((split, rows_a, LANES), f32),
+            pltpu.VMEM((split, rows_a, LANES), bf16),
+            pltpu.VMEM((split, plane, rows_b, LANES), bf16),
+            pltpu.VMEM((split, rows_b, LANES), f32),
+            pltpu.VMEM((split, line, rows_c, LANES), f32),
+            pltpu.VMEM((2, split, rows_a, LANES), bf16),
+            dma((2 * split,)),
+            dma((split,)), dma((split,)),
+            dma((split, plane)), dma((split, plane)),
+            dma((split, line)), dma((split, line)),
+            dma((split, line)), dma((split, line)),
+            dma((split, plane)), dma((split, plane)),
+            dma((split,)), dma((split,)),
+        ],
+        compiler_params=pltpu.CompilerParams(collective_id=1, has_side_effects=True),
+        name="reduce_terms",
+    )(embedded, cotangent)
+
 
 def body(token_ids, counts, table, projection, cotangent):
     tokens_here = token_ids.shape[0]
@@ -93,7 +295,7 @@
     before = (order[:, None] >= order[None, :]).astype(bf16)
     ranks = jnp.dot(before, hits, preferred_element_type=f32)
     rank = jnp.sum(ranks * hits.astype(f32), axis=1).astype(jnp.int32) - 1
-    slot_index = owner * capacity + rank
+    slot_index = jnp.where(order < counts[0], owner * capacity + rank, -1)
     place = (slot_index[:, None] == jnp.arange(slots, dtype=jnp.int32)[None, :]).astype(bf16)
     digits = jnp.stack(
         [local_row // 65536, (local_row // 256) % 256, local_row % 256, jnp.ones_like(local_row)]
@@ -108,10 +310,8 @@
     picked = jnp.where(valid[:, None], table[safe_rows], jnp.zeros((1, width), table.dtype))
     returned = exchange(picked.reshape(devices_all, capacity, width)).reshape(-1, width)
 
-    live = order < counts[0]
-    masked = jnp.where(live[:, None], cotangent, jnp.zeros_like(cotangent))
     token_grad = lax.dot_general(
-        masked, projection, (((1,), (1,)), ((), ())), preferred_element_type=f32
+        cotangent, projection, (((1,), (1,)), ((), ())), preferred_element_type=f32
     ).astype(bf16)
     outgoing = lax.dot_general(
         place, token_grad, (((0,), (0,)), ((), ())), preferred_element_type=f32
@@ -119,18 +319,11 @@
     incoming = exchange(outgoing.reshape(devices_all, capacity, width)).reshape(-1, width)
 
     embedded = jnp.dot(place, returned, preferred_element_type=f32).astype(bf16)
-    terms = lax.dot_general(
-        masked, embedded, (((0,), (0,)), ((), ())), preferred_element_type=f32
-    ).astype(bf16)
-    share = hidden_width // devices_all
-    parts = exchange(terms.reshape(devices_all, share, width))
     scaling = 1.0 / math.sqrt(tokens_here * devices_all)
-    summed = (jnp.sum(parts.astype(f32), axis=0) * scaling).astype(bf16)
-    spread = exchange(jnp.broadcast_to(summed[None], (devices_all, share, width)))
-    grad_projection = spread.reshape(hidden_width, width).T.astype(f32)
+    grad_projection = reduce_terms(embedded, cotangent, scaling).astype(f32)
 
     product = jnp.dot(embedded, projection, preferred_element_type=f32)
-    hidden = jnp.where(live[:, None], product, 0.0).astype(bf16)
+    hidden = product.astype(bf16)
     grad_table = scatter_rows(safe_rows, incoming.astype(f32), held_rows)
     return (hidden, grad_projection, grad_table)
 

time: 138 us -> 106 us (0.77)
  waiting for transfers between devices: 57.5 us -> 13.5 us
  Pallas kernels: 8.85 us -> 41.2 us
  blocking collectives: 13.6 us -> 0 us
  local copies, waits for them, and re-layouts: 12.2 us -> 7.05 us
  matrix products: 24.9 us -> 21 us
  starting transfers between devices: 12.5 us -> 16.2 us
    all_to_all x4 -> x3, waiting for transfers between devices: 57.5 us -> 13.5 us  [exchange(): return lax.all_to_all(blocks, AXES, split_axis=0, concat_axis=0, tiled=True)]
    pallas_call x0 -> x1, Pallas kernels: none -> 32.7 us  [reduce_terms(): pl.pallas_call(functools.partial(reduce_kernel, n_vocab, n_dp, split, sca...]
    all_to_all x1 -> x0, blocking collectives: 13.6 us -> none  [exchange(): return lax.all_to_all(blocks, AXES, split_axis=0, concat_axis=0, tiled=True)]
    dot_general x2 -> x0, matrix products: 13.3 us -> none  [the longest x1 7.29 us: body(): lax.dot_general(masked, embedded, (((0,), (0,)), ((), ())), preferred_ele...]
    dot_general x1, matrix products: 3.3 us -> 9.88 us  [body(): lax.dot_general(place, token_grad, (((0,), (0,)), ((), ())), preferred_el...]
    all_to_all x4 -> x3, starting transfers between devices: 12.5 us -> 16.2 us  [exchange(): return lax.all_to_all(blocks, AXES, split_axis=0, concat_axis=0, tiled=True)]
    unnamed x7 -> x10, local copies, waits for them, and re-layouts: 2.9 us -> 0.03 us
    dot_general x1, matrix products: 1.48 us -> 3.21 us  [body(): embedded = jnp.dot(place, returned, preferred_element_type=f32).astype(bf16)]
  transfers between devices with their start and end apart: 4 -> 3, of which waited for: 4 -> 2; matrix products, arithmetic and copies ran while one was open for 12% -> 17% of each run, Pallas kernels for 6% -> 8%
where the time goes in v2:
time: 106 us
  Pallas kernels  41.2 us (39%)
  matrix products  21 us (20%)
  starting transfers between devices  16.2 us (15%)
  waiting for transfers between devices  13.5 us (13%)
  local copies, waits for them, and re-layouts  7.05 us (7%)
  other arithmetic  5.22 us (5%)
  between operations  1.58 us (1%)
    pallas_call x1, Pallas kernels, reduce_terms(): pl.pallas_call(functools.partial(reduce_kernel, n_vocab, n_dp, split, sca...  32.7 us
    all_to_all x3, starting transfers between devices, exchange(): return lax.all_to_all(blocks, AXES, split_axis=0, concat_axis=0, tiled=True)  16.2 us
    all_to_all x3, waiting for transfers between devices, exchange(): return lax.all_to_all(blocks, AXES, split_axis=0, concat_axis=0, tiled=True)  13.5 us
    dot_general x1, matrix products, body(): lax.dot_general(place, token_grad, (((0,), (0,)), ((), ())), preferred_el...  9.88 us
    pallas_call x1, Pallas kernels, scatter_rows(): pl.pallas_call(functools.partial(scatter_kernel, chunks), out_shape=jax.S...  8.46 us
    gather x1, local copies, waits for them, and re-layouts, body(): table[safe_rows]  6.18 us
    dot_general x1, matrix products, body(): product = jnp.dot(embedded, projection, preferred_element_type=f32)  5.73 us
    dot_general x1, matrix products, body(): embedded = jnp.dot(place, returned, preferred_element_type=f32).astype(bf16)  3.21 us
  transfers between devices with their start and end apart: 3, of which 2 were waited for; matrix products, arithmetic and copies ran while one was open for 17% of the time, Pallas kernels for 8%

profile of v2, /device:TPU:1, one launch (start us, length us, event | category | flops | bytes accessed | tf_op | source)
XLA Modules:
  0.0 105.7 jit_solution(3546779471114730219)
XLA Ops:
  0.6 0.0 copy-start
  1.4 0.7 add_select_fusion.4
  2.1 0.5 fusion.11
  2.7 0.7 fusion.26
  3.4 0.1 pad.3.clone
  3.5 1.6 %fusion.8 = s32[4,2048]{1,0:T(4,128)S(1)} fusion(s32[1024]{0:T(1024)S(1)} %get-tuple-element.4, bf16[1,1024]{1,0:T(2,128)(2,1)S(1)} %stack.18, bf16[1,1024]{1,0:T(2,128)(2,1)S(1)} %stack.17, bf16[1,1024]{1,0:T(2,128)(2,1)S(1)} %stack.16, bf16[4]{0:T(256)(128)(2,1)S(1)} %pad.3.clone), kind=kOutput, calls=%fused_computation.12 | convolution fusion | flops 18915328 | bytes 43016 | tf_op jit(solution)/shard_map/dot_general | solution.py:303
  5.1 0.1 fusion.14
  5.2 0.7 reshape.132
  5.9 7.1 %all-to-all-start = ((s32[32,1,64]{2,1,0:T(1,128)}), s32[32,1,64]{2,1,0:T(1,128)S(1)}, u32[]{:S(2)}, u32[]{:S(2)}) async-start(s32[32,1,64]{2,1,0:T(1,128)} %bitcast.1), calls=%async_computation | async-start | bytes 32768 | tf_op jit(solution)/shard_map/all_to_all | solution.py:16
  13.0 9.9 %fusion.7 = bf16[2048,128]{1,0:T(8,128)(2,1)} fusion(s32[1024]{0:T(1024)S(1)} %get-tuple-element.4, bf16[1024,4096]{1,0:T(8,128)(2,1)} %cot_ref.1, bf16[128,4096]{1,0:T(8,128)(2,1)} %param.8), kind=kOutput, calls=%fused_computation.11 | convolution fusion | flops 1613103104 | bytes 9965568 | tf_op jit(solution)/shard_map/dot_general | solution.py:316
  22.8 0.0 all-to-all-done
  22.8 5.8 %all-to-all-start.2 = ((bf16[32,64,128]{2,1,0:T(8,128)(2,1)}), bf16[32,64,128]{2,1,0:T(8,128)(2,1)S(1)}, u32[]{:S(2)}, u32[]{:S(2)}) async-start(bf16[32,64,128]{2,1,0:T(8,128)(2,1)} %bitcast.7), calls=%async_computation.2 | async-start | bytes 1048576 | tf_op jit(solution)/shard_map/all_to_all | solution.py:16
  28.7 0.1 reshape.135.rows_ref
  28.8 0.0 copy-start.4
  28.8 0.0 copy-done
  28.8 6.2 %gather_fusion = bf16[2048,128]{1,0:T(8,128)(2,1)S(1)} fusion(bf16[8192,128]{1,0:T(8,128)(2,1)S(1)} %copy-done, s32[2048]{0:T(1024)S(1)} %broadcast_clamp_fusion), kind=kCustom, calls=%fused_computation | custom fusion | bytes 1056768 | tf_op jit(solution)/shard_map/gather | solution.py:310
  35.0 1.1 %broadcast_select_fusion = bf16[32,64,128]{2,1,0:T(8,128)(2,1)} fusion(bf16[32,64,128]{2,1,0:T(8,128)(2,1)S(1)} %bitcast.21, pred[32,64]{1,0:T(8,128)(4,1)S(1)} %compare_bitcast_fusion), kind=kLoop, calls=%fused_computation.18 | loop fusion | flops 262144 | bytes 1050624 | tf_op jit(solution)/shard_map/jit(_where)/select_n | solution.py:310
  36.1 7.8 %all-to-all-done.2 = bf16[32,64,128]{2,1,0:T(8,128)(2,1)S(1)} async-done(((bf16[32,64,128]{2,1,0:T(8,128)(2,1)}), bf16[32,64,128]{2,1,0:T(8,128)(2,1)S(1)}, u32[]{:S(2)}, u32[]{:S(2)}) %all-to-all-start.2) | async-done | bytes 524320 | tf_op jit(solution)/shard_map/all_to_all | solution.py:16
  43.9 3.3 %all-to-all-start.1 = ((bf16[32,64,128]{2,1,0:T(8,128)(2,1)}), bf16[32,64,128]{2,1,0:T(8,128)(2,1)}, u32[]{:S(2)}, u32[]{:S(2)}) async-start(bf16[32,64,128]{2,1,0:T(8,128)(2,1)} %broadcast_select_fusion), calls=%async_computation.1 | async-start | bytes 1048576 | tf_op jit(solution)/shard_map/all_to_all | solution.py:16
  47.2 1.1 %bitcast_convert_fusion.incoming_ref = f32[2048,128]{1,0:T(8,128)} fusion(bf16[32,64,128]{2,1,0:T(8,128)(2,1)S(1)} %all-to-all-done.2), kind=kLoop, calls=%fused_computation.17 | loop fusion | flops 262144 | bytes 1572864 | tf_op jit(solution)/shard_map/convert_element_type | solution.py:327
  48.3 0.0 copy-done.4
  48.3 8.5 %scatter_rows.1 = f32[8192,128]{1,0:T(8,128)} custom-call(s32[2048]{0:T(1024)} %copy-done.4, f32[2048,128]{1,0:T(8,128)} %bitcast_convert_fusion.incoming_ref), custom_call_target="tpu_custom_call" | custom-call | bytes 12582912 | tf_op jit(solution)/shard_map/scatter_rows/pallas_call | solution.py:64
  56.8 0.0 copy-start.3
  56.8 5.7 %all-to-all-done.1 = bf16[32,64,128]{2,1,0:T(8,128)(2,1)} async-done(((bf16[32,64,128]{2,1,0:T(8,128)(2,1)}), bf16[32,64,128]{2,1,0:T(8,128)(2,1)}, u32[]{:S(2)}, u32[]{:S(2)}) %all-to-all-start.1) | async-done | bytes 524320 | tf_op jit(solution)/shard_map/all_to_all | solution.py:16
  62.5 3.2 %fusion.9.emb_ref = bf16[1024,128]{1,0:T(8,128)(2,1)} fusion(bf16[2048,128]{1,0:T(8,128)(2,1)} %bitcast.6, s32[1024]{0:T(1024)S(1)} %get-tuple-element.4), kind=kOutput, calls=%fused_computation.13 | convolution fusion | flops 539099136 | bytes 790528 | tf_op jit(solution)/shard_map/dot_general | solution.py:321
  65.7 32.7 %reduce_terms.1 = bf16[128,4096]{1,0:T(8,128)(2,1)} custom-call(bf16[1024,128]{1,0:T(8,128)(2,1)} %fusion.9.emb_ref, bf16[1024,4096]{1,0:T(8,128)(2,1)} %cot_ref.1), custom_call_target="tpu_custom_call" | custom-call | tf_op jit(solution)/shard_map/reduce_terms/pallas_call | solution.py:249
  98.4 0.0 copy-done.3
  98.4 0.0 copy-done.2
  98.4 0.0 copy-start.1
  98.5 5.7 %convolution_convert_fusion = bf16[1024,4096]{1,0:T(8,128)(2,1)} fusion(bf16[1024,128]{1,0:T(8,128)(2,1)S(1)} %copy-done.2, bf16[128,4096]{1,0:T(8,128)(2,1)S(1)} %copy-done.3), kind=kOutput, calls=%fused_computation.5 | convolution fusion | flops 1077936128 | bytes 9699328 | tf_op jit(solution)/shard_map/dot_general | solution.py:325
  104.2 0.0 copy-done.1
  104.2 1.5 %convert_element_type.41 = f32[128,4096]{1,0:T(8,128)} convert(bf16[128,4096]{1,0:T(8,128)(2,1)S(1)} %copy-done.1) | non-fusion elementwise | flops 524288 | bytes 3145728 | tf_op jit(solution)/shard_map/convert_element_type | solution.py:323
  (7 shorter events, 0.0 us)
Async XLA Ops:
  0.6 28.1 %copy-start = (bf16[8192,128]{1,0:T(8,128)(2,1)S(1)}, bf16[8192,128]{1,0:T(8,128)(2,1)}, u32[]{:S(2)}) copy-start(bf16[8192,128]{1,0:T(8,128)(2,1)} %param.7) | copy-start | bytes 6291460
  5.9 17.0 %all-to-all-start = ((s32[32,1,64]{2,1,0:T(1,128)}), s32[32,1,64]{2,1,0:T(1,128)S(1)}, u32[]{:S(2)}, u32[]{:S(2)}) async-start(s32[32,1,64]{2,1,0:T(1,128)} %bitcast.1), calls=%async_computation | async-start | bytes 32768 | tf_op jit(solution)/shard_map/all_to_all | solution.py:16
  22.8 21.1 %all-to-all-start.2 = ((bf16[32,64,128]{2,1,0:T(8,128)(2,1)}), bf16[32,64,128]{2,1,0:T(8,128)(2,1)S(1)}, u32[]{:S(2)}, u32[]{:S(2)}) async-start(bf16[32,64,128]{2,1,0:T(8,128)(2,1)} %bitcast.7), calls=%async_computation.2 | async-start | bytes 1048576 | tf_op jit(solution)/shard_map/all_to_all | solution.py:16
  28.8 19.5 %copy-start.4 = (s32[2048]{0:T(1024)}, s32[2048]{0:T(1024)S(1)}, u32[]{:S(2)}) copy-start(s32[2048]{0:T(1024)S(1)} %reshape.135.rows_ref) | copy-start | bytes 24580
  43.9 18.5 %all-to-all-start.1 = ((bf16[32,64,128]{2,1,0:T(8,128)(2,1)}), bf16[32,64,128]{2,1,0:T(8,128)(2,1)}, u32[]{:S(2)}, u32[]{:S(2)}) async-start(bf16[32,64,128]{2,1,0:T(8,128)(2,1)} %broadcast_select_fusion), calls=%async_computation.1 | async-start | bytes 1048576 | tf_op jit(solution)/shard_map/all_to_all | solution.py:16
  56.8 41.7 %copy-start.3 = (bf16[128,4096]{1,0:T(8,128)(2,1)S(1)}, bf16[128,4096]{1,0:T(8,128)(2,1)}, u32[]{:S(2)}) copy-start(bf16[128,4096]{1,0:T(8,128)(2,1)} %param.8) | copy-start | bytes 3145732
  65.7 32.7 %copy-start.2 = (bf16[1024,128]{1,0:T(8,128)(2,1)S(1)}, bf16[1024,128]{1,0:T(8,128)(2,1)}, u32[]{:S(2)}) copy-start(bf16[1024,128]{1,0:T(8,128)(2,1)} %fusion.9.emb_ref) | copy-start | bytes 786436
  98.4 5.7 %copy-start.1 = (bf16[128,4096]{1,0:T(8,128)(2,1)S(1)}, bf16[128,4096]{1,0:T(8,128)(2,1)}, u32[]{:S(2)}) copy-start(bf16[128,4096]{1,0:T(8,128)(2,1)} %reduce_terms.1) | copy-start | bytes 3145732

commit v3 on v2

--- a/solution.py
+++ b/solution.py
@@ -87,7 +87,9 @@
 
 
 def reduce_kernel(
-    n_vocab, n_dp, split, scaling, emb_ref, cot_ref, out_ref,
+    n_vocab, n_dp, split, scaling,
+    picked_ref, slot_row, slot_col, proj_ref, cot_ref, out_ref, emb_ref, incoming_ref,
+    returned, outgoing, arrived, grad_sum, grad_half, rows_s, rows_r, grads_s, grads_r,
     cot_buf, emb_t, send_a, recv_a, acc_a, send_b, recv_b, acc_b, recv_c, full,
     load_sem, sa, ra, sb, rb, sc, rc, sd, rd, se, re, sf, rf,
 ):
@@ -118,10 +120,93 @@
 
     for j in range(2 * split):
         load(j).start()
+    devices_all = n_vocab * n_dp
+    me = v * n_dp + z
+    tokens = slot_row.shape[1]
+    slots = returned.shape[0]
+    capacity = slots // devices_all
     barrier = pltpu.get_barrier_semaphore()
-    peers = [partner] + [in_plane(k) for k in range(1, chips)] + [in_line(k) for k in range(1, n_dp)]
-    for where in peers:
-        pl.semaphore_signal(barrier, inc=1, device_id=where, device_id_type=MESH)
+
+    def device(k):
+        to = lax.rem(me + k, devices_all)
+        return to, (to // n_dp, lax.rem(to, n_dp))
+
+    def greet(k, carry):
+        pl.semaphore_signal(barrier, inc=1, device_id=device(k)[1], device_id_type=MESH)
+        return carry
+
+    def block(at):
+        return pl.ds(pl.multiple_of(at * capacity, capacity), capacity)
+
+    def copy_rows(k):
+        to, where = device(k)
+        return remote(
+            picked_ref.at[block(to), :], returned.at[block(me), :], rows_s.at[k], rows_r.at[k], where
+        )
+
+    def copy_grads(k):
+        to, where = device(k)
+        return remote(
+            outgoing.at[block(to), :], arrived.at[block(me), :], grads_s.at[k], grads_r.at[k], where
+        )
+
+    def each(action):
+        def step(k, carry):
+            action(k)
+            return carry
+
+        lax.fori_loop(1, devices_all, step, 0)
+
+    lax.fori_loop(1, devices_all, greet, 0)
+    pl.semaphore_wait(barrier, devices_all - 1)
+    each(lambda k: copy_rows(k).start())
+    returned[block(me), :] = picked_ref[block(me), :]
+
+    rows_tile = min(256, tokens)
+    for j in range(2 * split):
+        load(j).wait()
+        side = (1 - core) if j < split else core
+        at = pl.ds(pl.multiple_of(side * half + (j % split) * span, LANES), span)
+
+        def back(t, carry):
+            rows = pl.ds(pl.multiple_of(t * rows_tile, rows_tile), rows_tile)
+            y = lax.dot_general(
+                cot_buf[j, rows, :], proj_ref[:, at], (((1,), (1,)), ((), ())),
+                preferred_element_type=f32,
+            )
+            if j == 0:
+                grad_sum[rows, :] = y
+            else:
+                grad_sum[rows, :] = grad_sum[rows, :] + y
+            return carry
+
+        lax.fori_loop(0, tokens // rows_tile, back, 0)
+    grad_half[...] = grad_sum[...].astype(bf16)
+
+    slot_tile = 256
+
+    def spread(t, carry):
+        base = pl.multiple_of(t * slot_tile, slot_tile)
+        ids = lax.broadcasted_iota(jnp.int32, (slot_tile, tokens), 0) + base
+        place = jnp.where(ids == slot_row[...], 1.0, 0.0).astype(bf16)
+        y = jnp.dot(place, grad_half[...], preferred_element_type=f32)
+        outgoing[pl.ds(base, slot_tile), :] = y.astype(bf16)
+        return carry
+
+    lax.fori_loop(0, slots // slot_tile, spread, 0)
+    each(lambda k: copy_grads(k).start())
+    arrived[block(me), :] = outgoing[block(me), :]
+    each(lambda k: copy_rows(k).wait_recv())
+
+    def embed(t, carry):
+        rows = pl.ds(pl.multiple_of(t * rows_tile, rows_tile), rows_tile)
+        ids = lax.broadcasted_iota(jnp.int32, (rows_tile, slots), 1)
+        place = jnp.where(ids == slot_col[rows, :], 1.0, 0.0).astype(bf16)
+        y = jnp.dot(place, returned[...], preferred_element_type=f32)
+        emb_ref[rows, :] = y.astype(bf16)
+        return carry
+
+    lax.fori_loop(0, tokens // rows_tile, embed, 0)
     emb_t[...] = emb_ref[...].T
 
     def product(j, target):
@@ -167,13 +252,9 @@
         return remote(piece, piece, sf.at[q], rf.at[q], partner)
 
     for q in range(split):
-        load(q).wait()
         product(q, send_a.at[q])
-        if q == 0:
-            pl.semaphore_wait(barrier, len(peers))
         copy_a(q).start()
     for q in range(split):
-        load(split + q).wait()
         product(split + q, acc_a.at[q])
     plane = range(1, chips)
     line = range(1, n_dp)
@@ -222,6 +303,10 @@
     for q in range(split):
         copy_f(q).wait_recv()
         unpack(1 - core, q)
+    each(lambda k: copy_grads(k).wait_recv())
+    incoming_ref[...] = arrived[...].astype(f32)
+    each(lambda k: copy_rows(k).wait_send())
+    each(lambda k: copy_grads(k).wait_send())
     for q in range(split):
         copy_a(q).wait_send()
         copy_f(q).wait_send()
@@ -233,9 +318,11 @@
             copy_d(q, k).wait_send()
 
 
-def reduce_terms(embedded, cotangent, scaling):
+def reduce_terms(picked, slot_index, projection, cotangent, scaling):
     n_vocab, n_dp = lax.axis_size("vocab"), lax.axis_size("dp")
-    tokens, width = embedded.shape
+    tokens = slot_index.shape[0]
+    slots, width = picked.shape
+    devices_all = n_vocab * n_dp
     hidden_width = cotangent.shape[1]
     split = 2
     chips = n_vocab // 2
@@ -248,13 +335,22 @@
     plane, line = max(1, chips - 1), max(1, n_dp - 1)
     return pl.pallas_call(
         functools.partial(reduce_kernel, n_vocab, n_dp, split, scaling),
-        out_shape=jax.ShapeDtypeStruct((width, hidden_width), bf16),
-        in_specs=[
-            pl.BlockSpec(memory_space=pltpu.VMEM),
-            pl.BlockSpec(memory_space=pl.ANY),
+        out_shape=[
+            jax.ShapeDtypeStruct((width, hidden_width), bf16),
+            jax.ShapeDtypeStruct((tokens, width), bf16),
+            jax.ShapeDtypeStruct((slots, width), f32),
         ],
-        out_specs=pl.BlockSpec(memory_space=pltpu.VMEM),
+        in_specs=[pl.BlockSpec(memory_space=pltpu.VMEM)] * 4
+        + [pl.BlockSpec(memory_space=pl.ANY)],
+        out_specs=[pl.BlockSpec(memory_space=pltpu.VMEM)] * 3,
         scratch_shapes=[
+            pltpu.VMEM((slots, width), bf16),
+            pltpu.VMEM((slots, width), bf16),
+            pltpu.VMEM((slots, width), bf16),
+            pltpu.VMEM((tokens, width), f32),
+            pltpu.VMEM((tokens, width), bf16),
+            dma((devices_all,)), dma((devices_all,)),
+            dma((devices_all,)), dma((devices_all,)),
             pltpu.VMEM((2 * split, tokens, span), bf16),
             pltpu.VMEM((width, tokens), bf16),
             pltpu.VMEM((split, rows_a, LANES), bf16),
@@ -275,7 +371,7 @@
         ],
         compiler_params=pltpu.CompilerParams(collective_id=1, has_side_effects=True),
         name="reduce_terms",
-    )(embedded, cotangent)
+    )(picked, slot_index[None, :], slot_index[:, None], projection, cotangent)
 
 
 def body(token_ids, counts, table, projection, cotangent):
@@ -305,26 +401,16 @@
     requests = jnp.where(found[3] > 0, requests, -1)
 
     received = exchange(requests.reshape(devices_all, capacity)).reshape(-1)
-    valid = received >= 0
     safe_rows = jnp.maximum(received, 0)
-    picked = jnp.where(valid[:, None], table[safe_rows], jnp.zeros((1, width), table.dtype))
-    returned = exchange(picked.reshape(devices_all, capacity, width)).reshape(-1, width)
-
-    token_grad = lax.dot_general(
-        cotangent, projection, (((1,), (1,)), ((), ())), preferred_element_type=f32
-    ).astype(bf16)
-    outgoing = lax.dot_general(
-        place, token_grad, (((0,), (0,)), ((), ())), preferred_element_type=f32
-    ).astype(bf16)
-    incoming = exchange(outgoing.reshape(devices_all, capacity, width)).reshape(-1, width)
-
-    embedded = jnp.dot(place, returned, preferred_element_type=f32).astype(bf16)
     scaling = 1.0 / math.sqrt(tokens_here * devices_all)
-    grad_projection = reduce_terms(embedded, cotangent, scaling).astype(f32)
+    terms, embedded, incoming = reduce_terms(
+        table[safe_rows], slot_index, projection, cotangent, scaling
+    )
+    grad_projection = terms.astype(f32)
 
     product = jnp.dot(embedded, projection, preferred_element_type=f32)
     hidden = product.astype(bf16)
-    grad_table = scatter_rows(safe_rows, incoming.astype(f32), held_rows)
+    grad_table = scatter_rows(safe_rows, incoming, held_rows)
     return (hidden, grad_projection, grad_table)
 
 

time: 106 us -> 101 us (0.953)
  Pallas kernels: 41.2 us -> 64 us
  matrix products: 21 us -> 7.87 us
  starting transfers between devices: 16.2 us -> 7.09 us
  waiting for transfers between devices: 13.5 us -> 5.61 us
  local copies, waits for them, and re-layouts: 7.05 us -> 9.94 us
    pallas_call x1, Pallas kernels: 32.7 us -> 55.2 us  [reduce_terms(): pl.pallas_call(functools.partial(reduce_kernel, n_vocab, n_dp, split, sca...]
    dot_general x2 -> x0, matrix products: 13.1 us -> none  [the longest x1 9.88 us: body(): lax.dot_general(place, token_grad, (((0,), (0,)), ((), ())), preferred_el...]
    all_to_all x3 -> x1, starting transfers between devices: 16.2 us -> 7.09 us  [exchange(): return lax.all_to_all(blocks, AXES, split_axis=0, concat_axis=0, tiled=True)]
    all_to_all x3 -> x1, waiting for transfers between devices: 13.5 us -> 5.61 us  [exchange(): return lax.all_to_all(blocks, AXES, split_axis=0, concat_axis=0, tiled=True)]
    gather x1, local copies, waits for them, and re-layouts: 6.18 us -> 8.05 us  [body(): table[safe_rows]]
    select_n x1 -> x0, other arithmetic: 1.13 us -> none  [body(): jnp.where(valid[:, None], table[safe_rows], jnp.zeros((1, width), table.d...]
    convert_element_type x2 -> x1, other arithmetic: 2.6 us -> 2.86 us  [body(): grad_projection = terms.astype(f32)]
  transfers between devices with their start and end apart: 3 -> 1, of which waited for: 2 -> 1; matrix products, arithmetic and copies ran while one was open for 17% -> 1% of each run, Pallas kernels for 8% -> 0%
where the time goes in v3:
time: 101 us; the launch traced here: 100 us
  Pallas kernels  64 us (63%)
  local copies, waits for them, and re-layouts  9.94 us (10%)
  matrix products  7.87 us (8%)
  starting transfers between devices  7.09 us (7%)
  waiting for transfers between devices  5.61 us (6%)
  other arithmetic  4.38 us (4%)
  between operations  1.56 us (2%)
    pallas_call x1, Pallas kernels, reduce_terms(): pl.pallas_call(functools.partial(reduce_kernel, n_vocab, n_dp, split, sca...  55.2 us
    pallas_call x1, Pallas kernels, scatter_rows(): pl.pallas_call(functools.partial(scatter_kernel, chunks), out_shape=jax.S...  8.85 us
    gather x1, local copies, waits for them, and re-layouts, body(): table[safe_rows]  8.05 us
    all_to_all x1, starting transfers between devices, exchange(): return lax.all_to_all(blocks, AXES, split_axis=0, concat_axis=0, tiled=True)  7.09 us
    dot_general x1, matrix products, body(): product = jnp.dot(embedded, projection, preferred_element_type=f32)  5.73 us
    all_to_all x1, waiting for transfers between devices, exchange(): return lax.all_to_all(blocks, AXES, split_axis=0, concat_axis=0, tiled=True)  5.61 us
    convert_element_type x1, other arithmetic, body(): grad_projection = terms.astype(f32)  2.86 us
  transfers between devices with their start and end apart: 1, of which 1 were waited for; matrix products, arithmetic and copies ran while one was open for 1% of the time, Pallas kernels for 0%

profile of v3, /device:TPU:1, one launch (start us, length us, event | category | flops | bytes accessed | tf_op | source)
XLA Modules:
  0.0 100.5 jit_solution(7735025788957191263)
XLA Ops:
  0.6 0.0 copy-start
  1.4 0.7 add_select_fusion.4
  2.1 0.5 fusion.5
  2.7 0.7 fusion.20
  3.4 0.0 copy-start.4
  3.4 0.1 pad.3.clone
  3.5 1.6 %fusion.3 = s32[4,2048]{1,0:T(4,128)S(1)} fusion(s32[1024]{0:T(1024)S(1)} %get-tuple-element.10, bf16[1,1024]{1,0:T(2,128)(2,1)S(1)} %stack.18, bf16[1,1024]{1,0:T(2,128)(2,1)S(1)} %stack.17, bf16[1,1024]{1,0:T(2,128)(2,1)S(1)} %stack.16, bf16[4]{0:T(256)(128)(2,1)S(1)} %pad.3.clone), kind=kOutput, calls=%fused_computation.7 | convolution fusion | flops 18915328 | bytes 43016 | tf_op jit(solution)/shard_map/dot_general | solution.py:399
  5.1 0.1 fusion.8
  5.2 0.7 reshape.102
  5.9 7.1 %all-to-all-start = ((s32[32,1,64]{2,1,0:T(1,128)}), s32[32,1,64]{2,1,0:T(1,128)S(1)}, u32[]{:S(2)}, u32[]{:S(2)}) async-start(s32[32,1,64]{2,1,0:T(1,128)} %bitcast.1), calls=%async_computation | async-start | bytes 32768 | tf_op jit(solution)/shard_map/all_to_all | solution.py:16
  13.0 1.0 %copy.10.slot_col = s32[1024,1]{1,0:T(8,128)} copy(s32[1024,1]{0,1:T(1,128)S(1)} %bitcast.8) | data formatting | bytes 8192 | tf_op jit(solution)/shard_map/broadcast_in_dim | solution.py:395
  14.0 5.6 %all-to-all-done = s32[32,1,64]{2,1,0:T(1,128)S(1)} async-done(((s32[32,1,64]{2,1,0:T(1,128)}), s32[32,1,64]{2,1,0:T(1,128)S(1)}, u32[]{:S(2)}, u32[]{:S(2)}) %all-to-all-start) | async-done | bytes 8224 | tf_op jit(solution)/shard_map/all_to_all | solution.py:16
  19.6 0.1 maximum_reduce_fusion
  19.7 0.1 reshape.105.rows_ref
  19.7 0.0 copy-start.3
  19.7 0.0 copy-done
  19.7 8.1 %gather_fusion = bf16[2048,128]{1,0:T(8,128)(2,1)} fusion(bf16[8192,128]{1,0:T(8,128)(2,1)S(1)} %copy-done, s32[2048]{0:T(1024)S(1)} %broadcast_clamp_fusion), kind=kCustom, calls=%fused_computation | custom fusion | bytes 1056768 | tf_op jit(solution)/shard_map/gather | solution.py:407
  27.8 0.0 copy-done.4
  27.8 55.2 %reduce_terms.1 = (bf16[128,4096]{1,0:T(8,128)(2,1)}, bf16[1024,128]{1,0:T(8,128)(2,1)}, f32[2048,128]{1,0:T(8,128)}) custom-call(bf16[2048,128]{1,0:T(8,128)(2,1)} %gather_fusion, s32[1,1024]{1,0:T(1,128)} %bitcast.9, s32[1024,1]{1,0:T(8,128)} %copy.10.slot_col, bf16[128,4096]{1,0:T(8,128)(2,1)} %proj_ref.1, bf16[1024,4096]{1,0:T(8,128)(2,1)} %cot_ref.1), custom_call_target="tpu_custom_call" | custom-call | tf_op jit(solution)/shard_map/reduce_terms/pallas_call | solution.py:336
  83.0 0.0 copy-done.3
  83.0 0.0 copy-start.1
  83.0 0.0 copy-start.2
  83.0 2.9 %convert_element_type.26 = f32[128,4096]{1,0:T(8,128)} convert(bf16[128,4096]{1,0:T(8,128)(2,1)} %get-tuple-element.7) | non-fusion elementwise | flops 524288 | bytes 3145728 | tf_op jit(solution)/shard_map/convert_element_type | solution.py:409
  85.9 8.8 %scatter_rows.1 = f32[8192,128]{1,0:T(8,128)} custom-call(s32[2048]{0:T(1024)} %copy-done.3, f32[2048,128]{1,0:T(8,128)} %get-tuple-element.8.incoming_ref), custom_call_target="tpu_custom_call" | custom-call | bytes 12582912 | tf_op jit(solution)/shard_map/scatter_rows/pallas_call | solution.py:64
  94.7 0.0 copy-done.1
  94.7 0.0 copy-done.2
  94.7 5.7 %convolution_convert_fusion = bf16[1024,4096]{1,0:T(8,128)(2,1)} fusion(bf16[1024,128]{1,0:T(8,128)(2,1)S(1)} %copy-done.2, bf16[128,4096]{1,0:T(8,128)(2,1)S(1)} %copy-done.1), kind=kOutput, calls=%fused_computation.3 | convolution fusion | flops 1077936128 | bytes 9699328 | tf_op jit(solution)/shard_map/dot_general | solution.py:411
  (4 shorter events, 0.0 us)
Async XLA Ops:
  0.6 19.1 %copy-start = (bf16[8192,128]{1,0:T(8,128)(2,1)S(1)}, bf16[8192,128]{1,0:T(8,128)(2,1)}, u32[]{:S(2)}) copy-start(bf16[8192,128]{1,0:T(8,128)(2,1)} %param.7) | copy-start | bytes 6291460
  3.4 24.4 %copy-start.4 = (s32[1024]{0:T(1024)}, s32[1024]{0:T(1024)S(1)}, u32[]{:S(2)}) copy-start(s32[1024]{0:T(1024)S(1)} %get-tuple-element.10) | copy-start | bytes 12292
  5.9 13.7 %all-to-all-start = ((s32[32,1,64]{2,1,0:T(1,128)}), s32[32,1,64]{2,1,0:T(1,128)S(1)}, u32[]{:S(2)}, u32[]{:S(2)}) async-start(s32[32,1,64]{2,1,0:T(1,128)} %bitcast.1), calls=%async_computation | async-start | bytes 32768 | tf_op jit(solution)/shard_map/all_to_all | solution.py:16
  19.7 63.2 %copy-start.3 = (s32[2048]{0:T(1024)}, s32[2048]{0:T(1024)S(1)}, u32[]{:S(2)}) copy-start(s32[2048]{0:T(1024)S(1)} %reshape.105.rows_ref) | copy-start | bytes 24580
  83.0 11.7 %copy-start.1 = (bf16[128,4096]{1,0:T(8,128)(2,1)S(1)}, bf16[128,4096]{1,0:T(8,128)(2,1)}, u32[]{:S(2)}) copy-start(bf16[128,4096]{1,0:T(8,128)(2,1)} %proj_ref.1) | copy-start | bytes 3145732
  83.0 11.7 %copy-start.2 = (bf16[1024,128]{1,0:T(8,128)(2,1)S(1)}, bf16[1024,128]{1,0:T(8,128)(2,1)}, u32[]{:S(2)}) copy-start(bf16[1024,128]{1,0:T(8,128)(2,1)} %get-tuple-element.6) | copy-start | bytes 786436

commit v4 on v3

--- a/solution.py
+++ b/solution.py
@@ -10,10 +10,6 @@
 
 AXES = ("vocab", "dp")
 ACCS = 4
-
-
-def exchange(blocks):
-    return lax.all_to_all(blocks, AXES, split_axis=0, concat_axis=0, tiled=True)
 
 
 def scatter_kernel(chunks, rows_ref, incoming_ref, out_ref, acc0, acc1, acc2, acc3, sems):
@@ -88,7 +84,9 @@
 
 def reduce_kernel(
     n_vocab, n_dp, split, scaling,
-    picked_ref, slot_row, slot_col, proj_ref, cot_ref, out_ref, emb_ref, incoming_ref,
+    asked_ref, slot_row, slot_col, proj_ref, cot_ref, table_ref,
+    out_ref, emb_ref, incoming_ref, wanted_ref,
+    wanted, wanted_s, table_half, table_full, stage, picked, table_sem, want_sem, asks_s, asks_r,
     returned, outgoing, arrived, grad_sum, grad_half, rows_s, rows_r, grads_s, grads_r,
     cot_buf, emb_t, send_a, recv_a, acc_a, send_b, recv_b, acc_b, recv_c, full,
     load_sem, sa, ra, sb, rb, sc, rc, sd, rd, se, re, sf, rf,
@@ -118,6 +116,8 @@
         at = pl.ds(pl.multiple_of(side * half + (j % split) * span, LANES), span)
         return pltpu.make_async_copy(cot_ref.at[:, at], cot_buf.at[j], load_sem.at[j])
 
+    table_load = pltpu.make_async_copy(table_ref, table_half, table_sem)
+    table_load.start()
     for j in range(2 * split):
         load(j).start()
     devices_all = n_vocab * n_dp
@@ -138,10 +138,14 @@
     def block(at):
         return pl.ds(pl.multiple_of(at * capacity, capacity), capacity)
 
+    def copy_asks(k):
+        to, where = device(k)
+        return remote(asked_ref.at[to], wanted.at[me], asks_s.at[k], asks_r.at[k], where)
+
     def copy_rows(k):
         to, where = device(k)
         return remote(
-            picked_ref.at[block(to), :], returned.at[block(me), :], rows_s.at[k], rows_r.at[k], where
+            picked.at[block(to), :], returned.at[block(me), :], rows_s.at[k], rows_r.at[k], where
         )
 
     def copy_grads(k):
@@ -159,8 +163,37 @@
 
     lax.fori_loop(1, devices_all, greet, 0)
     pl.semaphore_wait(barrier, devices_all - 1)
-    each(lambda k: copy_rows(k).start())
-    returned[block(me), :] = picked_ref[block(me), :]
+    each(lambda k: copy_asks(k).start())
+    wanted[me] = asked_ref[me]
+    table_load.wait()
+    held_rows = table_half.shape[0]
+    wide = min(256, held_rows)
+
+    def widen(i, carry):
+        rows = pl.ds(pl.multiple_of(i * wide, wide), wide)
+        table_full[rows, :] = table_half[rows, :].astype(f32)
+        return carry
+
+    lax.fori_loop(0, held_rows // wide, widen, 0)
+    each(lambda k: copy_asks(k).wait_recv())
+    to_scalars = pltpu.make_async_copy(wanted, wanted_s, want_sem)
+    to_scalars.start()
+    to_scalars.wait()
+
+    def pick(at):
+        for i in range(capacity):
+            row = jnp.maximum(wanted_s[at, 0, i], 0)
+            stage[i : i + 1, :] = table_full[pl.ds(row, 1), :]
+        return stage[...].astype(bf16)
+
+    def serve(k):
+        at = device(k)[0]
+        picked[block(at), :] = pick(at)
+        copy_rows(k).start()
+
+    each(serve)
+    returned[block(me), :] = pick(me)
+    wanted_ref[...] = wanted[...]
 
     rows_tile = min(256, tokens)
     for j in range(2 * split):
@@ -305,6 +338,7 @@
         unpack(1 - core, q)
     each(lambda k: copy_grads(k).wait_recv())
     incoming_ref[...] = arrived[...].astype(f32)
+    each(lambda k: copy_asks(k).wait_send())
     each(lambda k: copy_rows(k).wait_send())
     each(lambda k: copy_grads(k).wait_send())
     for q in range(split):
@@ -318,11 +352,12 @@
             copy_d(q, k).wait_send()
 
 
-def reduce_terms(picked, slot_index, projection, cotangent, scaling):
+def reduce_terms(asked, slot_index, projection, cotangent, table, capacity, scaling):
     n_vocab, n_dp = lax.axis_size("vocab"), lax.axis_size("dp")
     tokens = slot_index.shape[0]
-    slots, width = picked.shape
+    held_rows, width = table.shape
     devices_all = n_vocab * n_dp
+    slots = devices_all * capacity
     hidden_width = cotangent.shape[1]
     split = 2
     chips = n_vocab // 2
@@ -339,11 +374,20 @@
             jax.ShapeDtypeStruct((width, hidden_width), bf16),
             jax.ShapeDtypeStruct((tokens, width), bf16),
             jax.ShapeDtypeStruct((slots, width), f32),
+            jax.ShapeDtypeStruct(asked.shape, jnp.int32),
         ],
         in_specs=[pl.BlockSpec(memory_space=pltpu.VMEM)] * 4
-        + [pl.BlockSpec(memory_space=pl.ANY)],
-        out_specs=[pl.BlockSpec(memory_space=pltpu.VMEM)] * 3,
+        + [pl.BlockSpec(memory_space=pl.ANY)] * 2,
+        out_specs=[pl.BlockSpec(memory_space=pltpu.VMEM)] * 4,
         scratch_shapes=[
+            pltpu.VMEM(asked.shape, jnp.int32),
+            pltpu.SMEM(asked.shape, jnp.int32),
+            pltpu.VMEM((held_rows, width), bf16),
+            pltpu.VMEM((held_rows, width), f32),
+            pltpu.VMEM((capacity, width), f32),
+            pltpu.VMEM((slots, width), bf16),
+            dma, dma,
+            dma((devices_all,)), dma((devices_all,)),
             pltpu.VMEM((slots, width), bf16),
             pltpu.VMEM((slots, width), bf16),
             pltpu.VMEM((slots, width), bf16),
@@ -371,7 +415,7 @@
         ],
         compiler_params=pltpu.CompilerParams(collective_id=1, has_side_effects=True),
         name="reduce_terms",
-    )(picked, slot_index[None, :], slot_index[:, None], projection, cotangent)
+    )(asked, slot_index[None, :], slot_index[:, None], projection, cotangent, table)
 
 
 def body(token_ids, counts, table, projection, cotangent):
@@ -400,12 +444,16 @@
     requests = found[0] * 65536 + found[1] * 256 + found[2] + found[3] - 1
     requests = jnp.where(found[3] > 0, requests, -1)
 
-    received = exchange(requests.reshape(devices_all, capacity)).reshape(-1)
-    safe_rows = jnp.maximum(received, 0)
+    asked = jnp.pad(
+        requests.reshape(devices_all, 1, capacity),
+        ((0, 0), (0, 0), (0, -capacity % LANES)),
+        constant_values=-1,
+    )
     scaling = 1.0 / math.sqrt(tokens_here * devices_all)
-    terms, embedded, incoming = reduce_terms(
-        table[safe_rows], slot_index, projection, cotangent, scaling
+    terms, embedded, incoming, wanted = reduce_terms(
+        asked, slot_index, projection, cotangent, table, capacity, scaling
     )
+    safe_rows = jnp.maximum(wanted[:, 0, :capacity].reshape(-1), 0)
     grad_projection = terms.astype(f32)
 
     product = jnp.dot(embedded, projection, preferred_element_type=f32)

time: 101 us -> 86.9 us (0.86)
  local copies, waits for them, and re-layouts: 9.94 us -> 2.5 us
  starting transfers between devices: 7.09 us -> 0 us
  Pallas kernels: 64 us -> 69.7 us
  waiting for transfers between devices: 5.61 us -> 0 us
    gather x1 -> x0, local copies, waits for them, and re-layouts: 8.05 us -> none  [body(): table[safe_rows]]
    all_to_all x1 -> x0, starting transfers between devices: 7.09 us -> none  [exchange(): return lax.all_to_all(blocks, AXES, split_axis=0, concat_axis=0, tiled=True)]
    pallas_call x1, Pallas kernels: 55.2 us -> 61.2 us  [reduce_terms(): pl.pallas_call(functools.partial(reduce_kernel, n_vocab, n_dp, split, sca...]
    all_to_all x1 -> x0, waiting for transfers between devices: 5.61 us -> none  [exchange(): return lax.all_to_all(blocks, AXES, split_axis=0, concat_axis=0, tiled=True)]
  transfers between devices with their start and end apart: 1 -> 0, of which waited for: 1 -> 0; matrix products, arithmetic and copies ran while one was open for 1% -> 0% of each run, Pallas kernels for 0% -> 0%
where the time goes in v4:
time: 86.9 us; the launch traced here: 86.5 us
  Pallas kernels  69.7 us (80%)
  matrix products  7.87 us (9%)
  other arithmetic  5.1 us (6%)
  local copies, waits for them, and re-layouts  2.5 us (3%)
  between operations  1.37 us (2%)
    pallas_call x1, Pallas kernels, reduce_terms(): pl.pallas_call(functools.partial(reduce_kernel, n_vocab, n_dp, split, sca...  61.2 us
    pallas_call x1, Pallas kernels, scatter_rows(): pl.pallas_call(functools.partial(scatter_kernel, chunks), out_shape=jax.S...  8.47 us
    dot_general x1, matrix products, body(): product = jnp.dot(embedded, projection, preferred_element_type=f32)  5.72 us
    convert_element_type x1, other arithmetic, body(): grad_projection = terms.astype(f32)  2.86 us

profile of v4, /device:TPU:1, one launch (start us, length us, event | category | flops | bytes accessed | tf_op | source)
XLA Modules:
  0.0 86.5 jit_solution(10487274781676358766)
XLA Ops:
  1.3 0.1 pad.8.clone
  1.4 0.7 add_select_fusion.4
  2.0 0.5 fusion.5
  2.6 0.7 fusion.20
  3.3 0.0 copy-start.2
  3.4 1.6 %fusion.3 = s32[4,2048]{1,0:T(4,128)S(1)} fusion(s32[1024]{0:T(1024)S(1)} %get-tuple-element.12, bf16[1,1024]{1,0:T(2,128)(2,1)S(1)} %stack.18, bf16[1,1024]{1,0:T(2,128)(2,1)S(1)} %stack.17, bf16[1,1024]{1,0:T(2,128)(2,1)S(1)} %stack.16, bf16[4]{0:T(256)(128)(2,1)S(1)} %pad.8.clone), kind=kOutput, calls=%fused_computation.6 | convolution fusion | flops 18915328 | bytes 43016 | tf_op jit(solution)/shard_map/dot_general | solution.py:443
  5.0 0.1 fusion.8
  5.0 0.1 reshape.81
  5.1 0.6 pad.4.asked_ref
  5.7 1.0 %copy.8.slot_col = s32[1024,1]{1,0:T(8,128)} copy(s32[1024,1]{0,1:T(1,128)S(1)} %bitcast.7) | data formatting | bytes 8192 | tf_op jit(solution)/shard_map/broadcast_in_dim | solution.py:439
  6.8 0.0 copy-done.2
  6.8 61.2 %reduce_terms.1 = (bf16[128,4096]{1,0:T(8,128)(2,1)}, bf16[1024,128]{1,0:T(8,128)(2,1)}, f32[2048,128]{1,0:T(8,128)}, s32[32,1,128]{2,1,0:T(1,128)}) custom-call(s32[32,1,128]{2,1,0:T(1,128)} %pad.4.asked_ref, s32[1,1024]{1,0:T(1,128)} %bitcast.8, s32[1024,1]{1,0:T(8,128)} %copy.8.slot_col, bf16[128,4096]{1,0:T(8,128)(2,1)} %proj_ref.1, ...), custom_call_target="tpu_custom_call" | custom-call | tf_op jit(solution)/shard_map/reduce_terms/pallas_call | solution.py:371
  68.0 0.8 maximum_reduce_fusion
  68.7 0.7 max.6.rows_ref
  69.4 0.0 copy-start
  69.4 0.0 copy-start.1
  69.4 2.9 %convert_element_type.26 = f32[128,4096]{1,0:T(8,128)} convert(bf16[128,4096]{1,0:T(8,128)(2,1)} %get-tuple-element.8) | non-fusion elementwise | flops 524288 | bytes 3145728 | tf_op jit(solution)/shard_map/convert_element_type | solution.py:457
  72.3 8.5 %scatter_rows.1 = f32[8192,128]{1,0:T(8,128)} custom-call(s32[2048]{0:T(1024)} %max.6.rows_ref, f32[2048,128]{1,0:T(8,128)} %get-tuple-element.10.incoming_ref), custom_call_target="tpu_custom_call" | custom-call | bytes 12582912 | tf_op jit(solution)/shard_map/scatter_rows/pallas_call | solution.py:60
  80.7 0.0 copy-done
  80.8 0.0 copy-done.1
  80.8 5.7 %convolution_convert_fusion = bf16[1024,4096]{1,0:T(8,128)(2,1)} fusion(bf16[1024,128]{1,0:T(8,128)(2,1)S(1)} %copy-done.1, bf16[128,4096]{1,0:T(8,128)(2,1)S(1)} %copy-done), kind=kOutput, calls=%fused_computation.2 | convolution fusion | flops 1077936128 | bytes 9699328 | tf_op jit(solution)/shard_map/dot_general | solution.py:459
  (3 shorter events, 0.0 us)
Async XLA Ops:
  3.3 3.4 %copy-start.2 = (s32[1024]{0:T(1024)}, s32[1024]{0:T(1024)S(1)}, u32[]{:S(2)}) copy-start(s32[1024]{0:T(1024)S(1)} %get-tuple-element.12) | copy-start | bytes 12292
  69.4 11.3 %copy-start = (bf16[128,4096]{1,0:T(8,128)(2,1)S(1)}, bf16[128,4096]{1,0:T(8,128)(2,1)}, u32[]{:S(2)}) copy-start(bf16[128,4096]{1,0:T(8,128)(2,1)} %proj_ref.1) | copy-start | bytes 3145732
  69.4 11.3 %copy-start.1 = (bf16[1024,128]{1,0:T(8,128)(2,1)S(1)}, bf16[1024,128]{1,0:T(8,128)(2,1)}, u32[]{:S(2)}) copy-start(bf16[1024,128]{1,0:T(8,128)(2,1)} %get-tuple-element.7) | copy-start | bytes 786436

commit v5 on v4

--- a/solution.py
+++ b/solution.py
@@ -12,34 +12,67 @@
 ACCS = 4
 
 
-def scatter_kernel(chunks, rows_ref, incoming_ref, out_ref, acc0, acc1, acc2, acc3, sems):
+def finish_kernel(
+    capacity, chunks, wanted_ref, incoming_ref, emb_ref, proj_ref, terms_ref,
+    table_out, hidden_out, proj_out,
+    acc0, acc1, acc2, acc3, hid, grad, table_sems, hidden_sems, proj_sem,
+):
+    f32, bf16 = jnp.float32, jnp.bfloat16
     accs = (acc0, acc1, acc2, acc3)
-    held = acc0.shape[0]
+    held, width = acc0.shape
     part = held // chunks
-    count = incoming_ref.shape[0]
+    slots = incoming_ref.shape[0]
+    tokens, hidden_width = hid.shape
+    high, wide = min(256, tokens), min(256, hidden_width)
+    blocks, tiles = tokens // high, hidden_width // wide
+    per = slots // (blocks * tiles)
+    group = min(8, per, capacity)
+
+    def convert(i, carry):
+        at = pl.ds(pl.multiple_of(i * wide, wide), wide)
+        grad[:, at] = terms_ref[:, at].astype(f32)
+        return carry
+
+    lax.fori_loop(0, tiles, convert, 0)
+    proj_copy = pltpu.make_async_copy(grad, proj_out, proj_sem)
+    proj_copy.start()
 
     def clear(i, carry):
         at = pl.ds(pl.multiple_of(i * 64, 64), 64)
         for acc in accs:
-            acc[at, :] = jnp.zeros((64, acc.shape[1]), jnp.float32)
+            acc[at, :] = jnp.zeros((64, width), f32)
         return carry
 
     lax.fori_loop(0, held // 64, clear, 0)
 
-    def add(i, carry):
-        base = pl.multiple_of(i * 8, 8)
-        block = incoming_ref[pl.ds(base, 8), :]
-        for j in range(8):
-            acc = accs[j % ACCS]
-            at = pl.ds(rows_ref[base + j], 1)
-            acc[at, :] = acc[at, :] + block[j : j + 1, :]
-        return carry
-
-    lax.fori_loop(0, count // 8, add, 0)
-
-    def copy(c):
+    def hidden_copy(r):
+        at = pl.ds(r * high, high)
+        return pltpu.make_async_copy(hid.at[at, :], hidden_out.at[at, :], hidden_sems.at[r])
+
+    for r in range(blocks):
+
+        def step(t, carry):
+            at = pl.ds(pl.multiple_of(t * wide, wide), wide)
+            y = jnp.dot(emb_ref[r * high : (r + 1) * high, :], proj_ref[:, at], preferred_element_type=f32)
+            start = (r * tiles + t) * per
+            for g in range(per // group):
+                base = pl.multiple_of(start + g * group, group)
+                block = incoming_ref[pl.ds(base, group), :]
+                source = base // capacity
+                first = lax.rem(base, capacity)
+                for j in range(group):
+                    acc = accs[j % ACCS]
+                    row = pl.ds(jnp.maximum(wanted_ref[source, 0, first + j], 0), 1)
+                    acc[row, :] = acc[row, :] + block[j : j + 1, :]
+            hid[r * high : (r + 1) * high, at] = y.astype(bf16)
+            return carry
+
+        lax.fori_loop(0, tiles, step, 0)
+        hidden_copy(r).start()
+
+    def table_copy(c):
         at = pl.ds(c * part, part)
-        return pltpu.make_async_copy(acc0.at[at, :], out_ref.at[at, :], sems.at[c])
+        return pltpu.make_async_copy(acc0.at[at, :], table_out.at[at, :], table_sems.at[c])
 
     for c in range(chunks):
 
@@ -49,27 +82,41 @@
             return carry
 
         lax.fori_loop(0, part // 64, join, 0)
-        copy(c).start()
+        table_copy(c).start()
+    proj_copy.wait()
+    for r in range(blocks):
+        hidden_copy(r).wait()
     for c in range(chunks):
-        copy(c).wait()
-
-
-def scatter_rows(rows, incoming, held_rows):
-    width = incoming.shape[1]
-    chunks = 4
+        table_copy(c).wait()
+
+
+def finish(wanted, incoming, embedded, projection, terms, held_rows, capacity):
+    tokens, width = embedded.shape
+    hidden_width = projection.shape[1]
+    chunks = 8
+    f32, bf16 = jnp.float32, jnp.bfloat16
+    dma = pltpu.SemaphoreType.DMA
     return pl.pallas_call(
-        functools.partial(scatter_kernel, chunks),
-        out_shape=jax.ShapeDtypeStruct((held_rows, width), jnp.float32),
-        in_specs=[
-            pl.BlockSpec(memory_space=pltpu.SMEM),
-            pl.BlockSpec(memory_space=pltpu.VMEM),
+        functools.partial(finish_kernel, capacity, chunks),
+        out_shape=[
+            jax.ShapeDtypeStruct((held_rows, width), f32),
+            jax.ShapeDtypeStruct((tokens, hidden_width), bf16),
+            jax.ShapeDtypeStruct((width, hidden_width), f32),
         ],
-        out_specs=pl.BlockSpec(memory_space=pl.ANY),
-        scratch_shapes=[pltpu.VMEM((held_rows, width), jnp.float32)] * ACCS
-        + [pltpu.SemaphoreType.DMA((chunks,))],
-        cost_estimate=pl.CostEstimate(flops=0, bytes_accessed=12 << 20, transcendentals=0),
-        name="scatter_rows",
-    )(rows, incoming)
+        in_specs=[pl.BlockSpec(memory_space=pltpu.SMEM)]
+        + [pl.BlockSpec(memory_space=pltpu.VMEM)] * 4,
+        out_specs=[pl.BlockSpec(memory_space=pl.ANY)] * 3,
+        scratch_shapes=[pltpu.VMEM((held_rows, width), f32)] * ACCS
+        + [
+            pltpu.VMEM((tokens, hidden_width), bf16),
+            pltpu.VMEM((width, hidden_width), f32),
+            dma((chunks,)),
+            dma((tokens // min(256, tokens),)),
+            dma,
+        ],
+        name="finish",
+    )(wanted, incoming, embedded, projection, terms)
+
 
 MESH = pl.DeviceIdType.MESH
 LANES = 128
@@ -453,12 +500,9 @@
     terms, embedded, incoming, wanted = reduce_terms(
         asked, slot_index, projection, cotangent, table, capacity, scaling
     )
-    safe_rows = jnp.maximum(wanted[:, 0, :capacity].reshape(-1), 0)
-    grad_projection = terms.astype(f32)
-
-    product = jnp.dot(embedded, projection, preferred_element_type=f32)
-    hidden = product.astype(bf16)
-    grad_table = scatter_rows(safe_rows, incoming, held_rows)
+    grad_table, hidden, grad_projection = finish(
+        wanted, incoming, embedded, projection, terms, held_rows, capacity
+    )
     return (hidden, grad_projection, grad_table)
 
 

time: 86.9 us -> 85.7 us (0.986)
  Pallas kernels: 69.7 us -> 78.7 us
  matrix products: 7.87 us -> 2.14 us
  other arithmetic: 5.1 us -> 1.47 us
    pallas_call x1, Pallas kernels: 8.47 us -> 17.5 us  [finish(): pl.pallas_call(functools.partial(finish_kernel, capacity, chunks), out_sh...]
    dot_general x1 -> x0, matrix products: 5.72 us -> none  [body(): product = jnp.dot(embedded, projection, preferred_element_type=f32)]
    convert_element_type x1 -> x0, other arithmetic: 2.86 us -> none  [body(): grad_projection = terms.astype(f32)]
where the time goes in v5:
time: 85.7 us; the launch traced here: 85.5 us
  Pallas kernels  78.7 us (92%)
  matrix products  2.14 us (2%)
  local copies, waits for them, and re-layouts  1.82 us (2%)
  other arithmetic  1.47 us (2%)
  between operations  1.34 us (2%)
    pallas_call x1, Pallas kernels, reduce_terms(): pl.pallas_call(functools.partial(reduce_kernel, n_vocab, n_dp, split, sca...  61.2 us
    pallas_call x1, Pallas kernels, finish(): pl.pallas_call(functools.partial(finish_kernel, capacity, chunks), out_sh...  17.5 us

profile of v5, /device:TPU:1, one launch (start us, length us, event | category | flops | bytes accessed | tf_op | source)
XLA Modules:
  0.0 85.5 jit_solution(6120348728135960929)
XLA Ops:
  1.3 0.1 pad.8.clone
  1.4 0.7 add_select_fusion.4
  2.0 0.5 fusion.5
  2.6 0.7 fusion.20
  3.3 0.0 copy-start
  3.4 1.6 %fusion.3 = s32[4,2048]{1,0:T(4,128)S(1)} fusion(s32[1024]{0:T(1024)S(1)} %get-tuple-element.18, bf16[1,1024]{1,0:T(2,128)(2,1)S(1)} %stack.18, bf16[1,1024]{1,0:T(2,128)(2,1)S(1)} %stack.17, bf16[1,1024]{1,0:T(2,128)(2,1)S(1)} %stack.16, bf16[4]{0:T(256)(128)(2,1)S(1)} %pad.8.clone), kind=kOutput, calls=%fused_computation.5 | convolution fusion | flops 18915328 | bytes 43016 | tf_op jit(solution)/shard_map/dot_general | solution.py:490
  5.0 0.1 fusion.8
  5.0 0.1 reshape.79
  5.1 0.6 pad.4.asked_ref
  5.7 1.0 %copy.8.slot_col = s32[1024,1]{1,0:T(8,128)} copy(s32[1024,1]{0,1:T(1,128)S(1)} %bitcast.5) | data formatting | bytes 8192 | tf_op jit(solution)/shard_map/broadcast_in_dim | solution.py:486
  6.8 0.0 copy-done
  6.8 61.2 %reduce_terms.1 = (bf16[128,4096]{1,0:T(8,128)(2,1)}, bf16[1024,128]{1,0:T(8,128)(2,1)}, f32[2048,128]{1,0:T(8,128)}, s32[32,1,128]{2,1,0:T(1,128)}) custom-call(s32[32,1,128]{2,1,0:T(1,128)} %pad.4.asked_ref, s32[1,1024]{1,0:T(1,128)} %bitcast.6, s32[1024,1]{1,0:T(8,128)} %copy.8.slot_col, bf16[128,4096]{1,0:T(8,128)(2,1)} %proj_ref.3, ...), custom_call_target="tpu_custom_call" | custom-call | tf_op jit(solution)/shard_map/reduce_terms/pallas_call | solution.py:418
  68.0 17.5 %finish.1 = (f32[8192,128]{1,0:T(8,128)}, bf16[1024,4096]{1,0:T(8,128)(2,1)}, f32[128,4096]{1,0:T(8,128)}) custom-call(s32[32,1,128]{2,1,0:T(1,128)} %get-tuple-element.10.wanted_ref, f32[2048,128]{1,0:T(8,128)} %get-tuple-element.11.incoming_ref, bf16[1024,128]{1,0:T(8,128)(2,1)} %get-tuple-element.12.emb_ref, bf16[128,4096]{1,0:T(8,128)(2,1)} %proj_ref.3, ...), custom_call_target="tpu_custom_call" | custom-call | tf_op jit(solution)/shard_map/finish/pallas_call | solution.py:99
  (3 shorter events, 0.0 us)
Async XLA Ops:
  3.3 3.4 %copy-start = (s32[1024]{0:T(1024)}, s32[1024]{0:T(1024)S(1)}, u32[]{:S(2)}) copy-start(s32[1024]{0:T(1024)S(1)} %get-tuple-element.18) | copy-start | bytes 12292

commit v6 on v5

--- a/solution.py
+++ b/solution.py
@@ -23,7 +23,7 @@
     part = held // chunks
     slots = incoming_ref.shape[0]
     tokens, hidden_width = hid.shape
-    high, wide = min(256, tokens), min(256, hidden_width)
+    high, wide = min(512, tokens), min(256, hidden_width)
     blocks, tiles = tokens // high, hidden_width // wide
     per = slots // (blocks * tiles)
     group = min(8, per, capacity)
@@ -111,7 +111,7 @@
             pltpu.VMEM((tokens, hidden_width), bf16),
             pltpu.VMEM((width, hidden_width), f32),
             dma((chunks,)),
-            dma((tokens // min(256, tokens),)),
+            dma((tokens // min(512, tokens),)),
             dma,
         ],
         name="finish",

time: 85.7 us -> 83.7 us (0.977)
  Pallas kernels: 78.7 us -> 76.7 us
    pallas_call x1, Pallas kernels: 17.5 us -> 15.5 us  [finish(): pl.pallas_call(functools.partial(finish_kernel, capacity, chunks), out_sh...]
where the time goes in v6:
time: 83.7 us; the launch traced here: 83.5 us
  Pallas kernels  76.7 us (92%)
  matrix products  2.14 us (3%)
  local copies, waits for them, and re-layouts  1.82 us (2%)
  other arithmetic  1.47 us (2%)
  between operations  1.34 us (2%)
    pallas_call x1, Pallas kernels, reduce_terms(): pl.pallas_call(functools.partial(reduce_kernel, n_vocab, n_dp, split, sca...  61.2 us
    pallas_call x1, Pallas kernels, finish(): pl.pallas_call(functools.partial(finish_kernel, capacity, chunks), out_sh...  15.5 us

profile of v6, /device:TPU:1, one launch (start us, length us, event | category | flops | bytes accessed | tf_op | source)
XLA Modules:
  0.0 83.5 jit_solution(5482350023360881680)
XLA Ops:
  1.3 0.1 pad.8.clone
  1.4 0.7 add_select_fusion.4
  2.0 0.5 fusion.5
  2.6 0.7 fusion.20
  3.3 0.0 copy-start
  3.4 1.6 %fusion.3 = s32[4,2048]{1,0:T(4,128)S(1)} fusion(s32[1024]{0:T(1024)S(1)} %get-tuple-element.18, bf16[1,1024]{1,0:T(2,128)(2,1)S(1)} %stack.18, bf16[1,1024]{1,0:T(2,128)(2,1)S(1)} %stack.17, bf16[1,1024]{1,0:T(2,128)(2,1)S(1)} %stack.16, bf16[4]{0:T(256)(128)(2,1)S(1)} %pad.8.clone), kind=kOutput, calls=%fused_computation.5 | convolution fusion | flops 18915328 | bytes 43016 | tf_op jit(solution)/shard_map/dot_general | solution.py:490
  5.0 0.1 fusion.8
  5.0 0.1 reshape.79
  5.1 0.6 pad.4.asked_ref
  5.7 1.0 %copy.8.slot_col = s32[1024,1]{1,0:T(8,128)} copy(s32[1024,1]{0,1:T(1,128)S(1)} %bitcast.5) | data formatting | bytes 8192 | tf_op jit(solution)/shard_map/broadcast_in_dim | solution.py:486
  6.8 0.0 copy-done
  6.8 61.2 %reduce_terms.1 = (bf16[128,4096]{1,0:T(8,128)(2,1)}, bf16[1024,128]{1,0:T(8,128)(2,1)}, f32[2048,128]{1,0:T(8,128)}, s32[32,1,128]{2,1,0:T(1,128)}) custom-call(s32[32,1,128]{2,1,0:T(1,128)} %pad.4.asked_ref, s32[1,1024]{1,0:T(1,128)} %bitcast.6, s32[1024,1]{1,0:T(8,128)} %copy.8.slot_col, bf16[128,4096]{1,0:T(8,128)(2,1)} %proj_ref.3, ...), custom_call_target="tpu_custom_call" | custom-call | tf_op jit(solution)/shard_map/reduce_terms/pallas_call | solution.py:418
  68.0 15.5 %finish.1 = (f32[8192,128]{1,0:T(8,128)}, bf16[1024,4096]{1,0:T(8,128)(2,1)}, f32[128,4096]{1,0:T(8,128)}) custom-call(s32[32,1,128]{2,1,0:T(1,128)} %get-tuple-element.10.wanted_ref, f32[2048,128]{1,0:T(8,128)} %get-tuple-element.11.incoming_ref, bf16[1024,128]{1,0:T(8,128)(2,1)} %get-tuple-element.12.emb_ref, bf16[128,4096]{1,0:T(8,128)(2,1)} %proj_ref.3, ...), custom_call_target="tpu_custom_call" | custom-call | tf_op jit(solution)/shard_map/finish/pallas_call | solution.py:99
  (3 shorter events, 0.0 us)
Async XLA Ops:
  3.3 3.4 %copy-start = (s32[1024]{0:T(1024)}, s32[1024]{0:T(1024)S(1)}, u32[]{:S(2)}) copy-start(s32[1024]{0:T(1024)S(1)} %get-tuple-element.18) | copy-start | bytes 12292
